TPU v7x, 256 devices: a whole 4x4x8 slice. The times are simulated.
256 devices in a mesh: row: 8 (over z_hi, x), col: 32 (over z_lo, y, core).
Axes of the slice: x: 4, y: 4, z: 8 (z_hi: 2, z_lo: 4; z = z_hi * 4 + z_lo), core: 2. Of those that a mesh axis runs over, the one named last changes fastest.
Arguments:
- object_field: float32 [2, 2048, 8192], P(None, 'row', 'col'), may hold values from -6 to 6
- probe: float32 [2, 4, 128, 128], replicated, may hold values from -6 to 6
- patterns: bfloat16 [8, 32, 8, 128, 128], P('row', 'col'), may hold values from 0.5 to 2
- row_scales: float32 [8, 32, 8, 128], P('row', 'col'), may hold values from 0.3 to 3
- positions: int32 [8, 32, 8, 2], P('row', 'col'), may hold values from 0 to 255
- counts: int32 [8, 32], P('row', 'col'), may hold values from 4 to 8, as said below
Outputs:
- object_out: float32 [2, 2048, 8192], P(None, 'row', 'col')
- probe_out: float32 [2, 4, 128, 128], replicated
Inputs may be any that keep to these rules, and one draw needn't show every extreme that they name: positions p >= counts[a,b] of tile (a,b) are ignored; some tile has all 8 positions live.
All inputs are finite; a program needn't handle non-finite values.
Results may differ from a plain program's by a relative error of at most 0.0003.
Values sent between devices are 32-bit elements; how exact they have to be, the bound alone decides.
No kernel may reach another device: no remote copies, remote signals or barrier semaphores. Data moves between devices by JAX's collectives and lax.ppermute only.
A program may use at most 128 MiB of HBM per device.

v0:
```python
import functools

import numpy as np

import jax
import jax.numpy as jnp
from jax import lax
from jax.experimental import pallas as pl
from jax.experimental.pallas import tpu as pltpu
from jax.sharding import PartitionSpec as P


LANES = 128
SUBLANES = 8
CORES = 2
TOGETHER = 4


def dft_tables(length):
    index = np.arange(length)
    angle = (np.outer(index, index) % length) * (2.0 * np.pi / length)
    cosine = np.cos(angle) / np.sqrt(length)
    sine = np.sin(angle) / np.sqrt(length)
    forward = np.block([[cosine, -sine], [sine, cosine]]).astype(np.float32)
    high = forward.astype(jnp.bfloat16)
    low = (forward - high.astype(np.float32)).astype(jnp.bfloat16)
    return high, low, np.ascontiguousarray(high.T), np.ascontiguousarray(low.T)


def split(value):
    high = value.astype(jnp.bfloat16)
    low = (value - high.astype(jnp.float32)).astype(jnp.bfloat16)
    return high, low


def mm(left, right):
    return jnp.dot(left, right, preferred_element_type=jnp.float32)


def product(left, right):
    (lh, ll), (rh, rl) = left, right
    return mm(lh, rh) + (mm(lh, rl) + mm(ll, rh))


def pass_kernel(*refs, modes, size, margin, renew):
    if renew:
        starts, counts, core, frame, old_probe, mean_mine, mean_other, amplitude, *refs = refs
        fh, fl, ih, il, updates, mine, other, probe, sums = refs
        half_rows = mean_mine.shape[0]
        sums[pl.ds(pl.multiple_of(core[0] * half_rows, size), half_rows)] = mean_mine[...]
        sums[pl.ds(pl.multiple_of((1 - core[0]) * half_rows, size), half_rows)] = mean_other[...]
        weight = sums[pl.ds(2 * modes * size, size)]
        for part in range(2):
            for m in range(modes):
                step = sums[pl.ds((part * modes + m) * size, size)] / weight
                probe[part, m] = old_probe[part, m] + step
    else:
        starts, counts, core, frame, probe, amplitude, *refs = refs
        fh, fl, ih, il, updates, mine, other, sums = refs
    updates[...] = jnp.zeros_like(updates)
    sums[...] = jnp.zeros_like(sums)
    forward = (fh[...], fl[...])
    inverse = (ih[...], il[...])

    tall, wide = size + SUBLANES, 2 * size

    def window(p):
        row = starts[p, 0]
        col = starts[p, 1] + margin
        rows = pl.ds(pl.multiple_of(row // SUBLANES * SUBLANES, SUBLANES), tall)
        cols = pl.ds(pl.multiple_of(col // LANES * LANES, LANES), wide)
        return rows, cols, row % SUBLANES, col % LANES

    def cut(part, place):
        rows, cols, down, shift = place
        block = pltpu.roll(frame[part, rows, cols], lax.rem(wide - shift, wide), 1)[:, :size]
        return pltpu.roll(block, lax.rem(tall - down, tall), 0)[:size]

    def add(part, place, patch):
        rows, cols, down, shift = place
        patch = jnp.concatenate([patch, jnp.zeros((SUBLANES, size), jnp.float32)], axis=0)
        patch = pltpu.roll(patch, down, 0)
        patch = pltpu.roll(jnp.concatenate([patch, jnp.zeros_like(patch)], axis=1), shift, 1)
        updates[part, rows, cols] += patch

    def exits(patch):
        re, im = patch
        waves = []
        for m in range(modes):
            pr, pi = probe[0, m], probe[1, m]
            waves.append((pr * re - pi * im, pr * im + pi * re))
        return waves

    def along_rows(waves, table):
        stacked = jnp.concatenate([jnp.concatenate(w, axis=1) for w in waves], axis=0)
        return product(split(stacked), table)

    def side(half):
        blocks = [half[m * size : (m + 1) * size] for m in range(modes)]
        return jnp.concatenate(
            [jnp.concatenate([b[:, :size], b[:, size:]], axis=0) for b in blocks], axis=1
        )

    def scale(far, p):
        squares = far * far
        power = squares[:size] + squares[size:]
        intensity = power[:, :size]
        for m in range(1, modes):
            intensity = intensity + power[:, m * size : (m + 1) * size]
        factor = amplitude[p] / jnp.maximum(jnp.sqrt(intensity), 0.5)
        factor = jnp.concatenate([factor] * modes, axis=1)
        return far * jnp.concatenate([factor, factor], axis=0)

    def columns(half):
        return [
            (half[:size, m * size : (m + 1) * size], half[size:, m * size : (m + 1) * size])
            for m in range(modes)
        ]

    def several(step, carry):
        ps = [step * TOGETHER + k for k in range(TOGETHER)]
        ps = [jnp.minimum(p, last) for p in ps]
        live = [jnp.where(step * TOGETHER + k <= last, 1.0, 0.0) for k in range(TOGETHER)]
        places = [window(p) for p in ps]
        patches = [(cut(0, place), cut(1, place)) for place in places]
        halves = [along_rows(exits(patch), forward) for patch in patches]
        fars = [product(inverse, split(side(half))) for half in halves]
        halves = [product(forward, split(scale(far, p))) for far, p in zip(fars, ps)]
        backs = [along_rows(columns(half), inverse) for half in halves]
        differences = []
        for patch, back, on in zip(patches, backs, live):
            waves = exits(patch)
            differences.append(
                [
                    (
                        (back[m * size : (m + 1) * size, :size] - waves[m][0]) * on,
                        (back[m * size : (m + 1) * size, size:] - waves[m][1]) * on,
                    )
                    for m in range(modes)
                ]
            )
        for m in range(modes):
            g_re = g_im = None
            for (re, im), difference in zip(patches, differences):
                dr, di = difference[m]
                one_re, one_im = re * dr + im * di, re * di - im * dr
                g_re = one_re if g_re is None else g_re + one_re
                g_im = one_im if g_im is None else g_im + one_im
            sums[pl.ds(m * size, size)] += g_re
            sums[pl.ds((modes + m) * size, size)] += g_im
        weight = None
        for (re, im), on in zip(patches, live):
            one = (re * re + im * im) * on
            weight = one if weight is None else weight + one
        sums[pl.ds(2 * modes * size, size)] += weight
        for place, difference in zip(places, differences):
            total_re = total_im = None
            for m in range(modes):
                pr, pi = probe[0, m], probe[1, m]
                dr, di = difference[m]
                one_re, one_im = pr * dr + pi * di, pr * di - pi * dr
                total_re = one_re if m == 0 else total_re + one_re
                total_im = one_im if m == 0 else total_im + one_im
            add(0, place, total_re)
            add(1, place, total_im)
        return carry

    last = counts[0] - 1
    lax.fori_loop(0, (counts[0] + TOGETHER - 1) // TOGETHER, several, 0)
    strength = probe[0, 0] * probe[0, 0] + probe[1, 0] * probe[1, 0]
    for m in range(1, modes):
        strength = strength + probe[0, m] * probe[0, m] + probe[1, m] * probe[1, m]
    updates[...] = updates[...] / jnp.max(strength)
    half_rows = mine.shape[0]
    mine[...] = sums[pl.ds(pl.multiple_of(core[0] * half_rows, size), half_rows)]
    other[...] = sums[pl.ds(pl.multiple_of((1 - core[0]) * half_rows, size), half_rows)]


def run_pass(starts, count, core, frame, probe, means, amplitude, tables, margin):
    modes, size = probe.shape[1], probe.shape[2]
    renew = means is not None
    half_rows = (modes + 1) * size
    vmem = pl.BlockSpec(memory_space=pltpu.VMEM)
    smem = pl.BlockSpec(memory_space=pltpu.SMEM)
    flops = 24 * starts.shape[0] * modes * size * (2 * size) ** 2
    half = jax.ShapeDtypeStruct((half_rows, size), jnp.float32)
    shapes = [jax.ShapeDtypeStruct(frame.shape, jnp.float32), half, half]
    if renew:
        shapes.append(jax.ShapeDtypeStruct(probe.shape, jnp.float32))
    operands = [frame, probe, *(means or ()), amplitude, *tables]
    return pl.pallas_call(
        functools.partial(pass_kernel, modes=modes, size=size, margin=margin, renew=renew),
        out_shape=shapes,
        in_specs=[smem] * 3 + [vmem] * len(operands),
        out_specs=[vmem] * len(shapes),
        scratch_shapes=[pltpu.VMEM((2 * half_rows, size), jnp.float32)],
        cost_estimate=pl.CostEstimate(flops=flops, bytes_accessed=6 << 20, transcendentals=0),
        compiler_params=pltpu.CompilerParams(vmem_limit_bytes=48 << 20),
    )(starts, count, core, *operands)


def neighbours(low_strip, high_strip, axis):
    count = lax.axis_size(axis)
    odd = lax.axis_index(axis) % 2 == 1

    def meet(block, start):
        pairs = [(i, i + 1) for i in range(start, count - 1, 2)]
        return lax.ppermute(block, axis, pairs + [(j, i) for i, j in pairs])

    first = meet(jnp.where(odd, high_strip, low_strip), 1)
    second = meet(jnp.where(odd, low_strip, high_strip), 0)
    return jnp.where(odd, second, first), jnp.where(odd, first, second)


AXES = ("row", "col")


def groups(row_step, col_step):
    n_row, n_col = lax.axis_size("row"), lax.axis_size("col")

    def flat(zh, x, zl, yc):
        return (zh * row_step + x) * n_col + zl * col_step + yc

    z = [(zh, zl) for zh in range(n_row // row_step) for zl in range(n_col // col_step)]
    planes = [
        [flat(zh, x, zl, y * CORES + c) for x in range(row_step) for y in range(col_step // CORES)]
        for zh, zl in z
        for c in range(CORES)
    ]
    lines = [[flat(zh, x, zl, yc) for zh, zl in z] for x in range(row_step) for yc in range(col_step)]
    return planes, lines


def exchange(blocks, members):
    return lax.all_to_all(blocks, AXES, 0, 0, axis_index_groups=members, tiled=True)


def spread(chunk, members):
    return exchange(jnp.broadcast_to(chunk[None], (len(members[0]), *chunk.shape)), members)


def swap(block):
    count = lax.axis_size("col")
    return lax.ppermute(block, "col", [(i, i ^ 1) for i in range(count)])


def total(mine, other):
    planes, lines = groups(4, 8)
    mine = mine + swap(other)
    parts = exchange(mine.reshape(len(planes[0]), -1, LANES), planes)
    part = jnp.sum(spread(jnp.sum(parts, axis=0), lines), axis=0)
    mine = spread(part, planes).reshape(mine.shape)
    return mine, swap(mine)


def at(array, dim, start, stop):
    return lax.slice_in_dim(array, start, stop, axis=dim)


def padded(array, dim, low, size):
    pads = [(0, 0, 0)] * array.ndim
    pads[dim] = (low, size - low - array.shape[dim], 0)
    return lax.pad(array, jnp.float32(0), pads)


def on_device(object_field, probe, patterns, row_scales, positions, counts):
    modes, size = probe.shape[1], probe.shape[2]
    rim = size // 2
    rows, cols = object_field.shape[1:]
    tall, wide = rows + 2 * rim, cols + 2 * LANES
    margin = LANES - rim
    tables = [jnp.asarray(t) for t in dft_tables(size)]
    amplitude = patterns[0, 0].astype(jnp.float32) * row_scales[0, 0][..., None]
    starts, count = positions[0, 0], counts[0]

    low, high = neighbours(at(object_field, 1, 0, rim), at(object_field, 1, rows - rim, rows), "row")
    frame = jnp.concatenate([low, object_field, high], axis=1)
    low, high = neighbours(at(frame, 2, 0, LANES), at(frame, 2, cols - LANES, cols), "col")
    frame = jnp.concatenate([low, frame, high], axis=2)

    at_row = lax.broadcasted_iota(jnp.int32, (1, tall, 1), 1) + (lax.axis_index("row") * rows - rim)
    at_col = lax.broadcasted_iota(jnp.int32, (1, 1, wide), 2) + (lax.axis_index("col") * cols - LANES)
    inside = (at_row >= 0) & (at_row < rows * lax.axis_size("row"))
    inside = inside & (at_col >= 0) & (at_col < cols * lax.axis_size("col"))
    core = (lax.axis_index("col") % CORES).reshape(1)
    left, right = margin, LANES + cols + rim
    updates, mine, other = run_pass(starts, count, core, frame, probe, None, amplitude, tables, margin)
    means = total(mine, other)
    strips = at(updates, 2, left, right)
    low, high = neighbours(at(strips, 2, 0, 2 * rim), at(strips, 2, cols, cols + 2 * rim), "col")
    strips = strips + padded(low, 2, 0, cols + 2 * rim) + padded(high, 2, cols, cols + 2 * rim)
    low, high = neighbours(at(strips, 1, 0, 2 * rim), at(strips, 1, rows, tall), "row")
    strips = strips + padded(low, 1, 0, tall) + padded(high, 1, rows, tall)
    updates = padded(strips, 2, left, wide)
    frame = frame + jnp.where(inside, updates, 0.0)

    updates, mine, other, probe = run_pass(
        starts, count, core, frame, probe, means, amplitude, tables, margin
    )
    mine, other = total(mine, other)
    strips = at(updates, 2, left, right)
    low, high = neighbours(at(strips, 2, 0, rim), at(strips, 2, rim + cols, cols + 2 * rim), "col")
    middle = at(strips, 2, rim, rim + cols)
    middle = middle + padded(low, 2, 0, cols) + padded(high, 2, cols - rim, cols)
    low, high = neighbours(at(middle, 1, 0, rim), at(middle, 1, tall - rim, tall), "row")
    tile = at(middle, 1, rim, rim + rows)
    tile = tile + padded(low, 1, 0, rows) + padded(high, 1, rows - rim, rows)
    object_out = frame[:, rim : rim + rows, LANES : LANES + cols] + tile
    lower = jnp.where(core[0] == 0, mine, other)
    upper = jnp.where(core[0] == 0, other, mine)
    sums = jnp.concatenate([lower, upper]).reshape(-1, size, size)
    probe_out = probe + sums[: 2 * modes].reshape(probe.shape) / sums[2 * modes]
    return object_out, probe_out


def solution(mesh):
    placed = (
        P(None, "row", "col"),
        P(),
        P("row", "col", None, None, None),
        P("row", "col", None, None),
        P("row", "col", None, None),
        P("row", "col"),
    )
    return jax.shard_map(
        on_device,
        mesh=mesh,
        in_specs=placed,
        out_specs=(P(None, "row", "col"), P()),
        check_vma=False,
    )
```

profile of v0, /device:TPU:6, one launch (start us, length us, event | category | flops | bytes accessed | tf_op | source)
XLA Modules:
  0.0 175.4 jit_solution(18227807363400343411)
XLA Ops:
  2.6 9.7 %collective-permute-start.1 = (f32[2,64,256]{2,1,0:T(8,128)S(1)}, f32[2,64,256]{2,1,0:T(8,128)S(1)}, u32[]{:S(2)}, u32[]{:S(2)}) collective-permute-start(f32[2,64,256]{2,1,0:T(8,128)S(1)} %get-tuple-element.37), channel_id=1, source_target_pairs={{32,64},{96,128},{160,192},{64,32},{128,96},{192,160},{33,65},{97,... | collective-permute-start | bytes 393224 | tf_op jit(solution)/shard_map/ppermute | solution.py:208
  12.3 3.3 %collective-permute-done.1 = f32[2,64,256]{2,1,0:T(8,128)S(1)} collective-permute-done((f32[2,64,256]{2,1,0:T(8,128)S(1)}, f32[2,64,256]{2,1,0:T(8,128)S(1)}, u32[]{:S(2)}, u32[]{:S(2)}) %collective-permute-start.1) | collective-permute-done | bytes 131104 | tf_op jit(solution)/shard_map/ppermute | solution.py:208
  20.4 10.2 %shard_map.113 = (f32[2,384,512]{2,1,0:T(8,128)S(1)}, f32[640,128]{1,0:T(8,128)S(1)}, f32[640,128]{1,0:T(8,128)S(1)}) custom-call(s32[8,2]{1,0:T(8,128)S(1)} %copy.14.refs_0_, s32[1]{0:T(128)} %bitcast.14.refs_1_, s32[1]{0:T(128)} %bitcast.2.refs_2_, f32[2,384,512]{2,1,0:T(8,128)S(1)} %pad_maximum_fusion.refs_3_, f32[2,4,128,128]{3,2,1,0:T(8,128)S(1)} %copy-done, ...), custom_call_target="tpu_custom_call" | custom-call | flops 6442450944 | bytes 6291456 | tf_op jit(solution)/shard_map/pallas_call | solution.py:191
  31.7 7.8 %collective-permute-start.4 = (f32[2,384,128]{2,1,0:T(8,128)}, f32[2,384,128]{2,1,0:T(8,128)}, u32[]{:S(2)}, u32[]{:S(2)}) collective-permute-start(f32[2,384,128]{2,1,0:T(8,128)} %get-tuple-element.18), channel_id=1, source_target_pairs={{0,1},{2,3},{4,5},{6,7},{8,9},{10,11},{12,13},{14,15},{16,17},{18,... | collective-permute-start | bytes 1179656 | tf_op jit(solution)/shard_map/ppermute | solution.py:208
  39.5 1.4 collective-permute-start.5
  40.9 2.3 %collective-permute-start.8 = (f32[640,128]{1,0:T(8,128)S(1)}, f32[640,128]{1,0:T(8,128)}, u32[]{:S(2)}, u32[]{:S(2)}) collective-permute-start(f32[640,128]{1,0:T(8,128)S(1)} %get-tuple-element.11), channel_id=1, source_target_pairs={{0,1},{1,0},{2,3},{3,2},{4,5},{5,4},{6,7},{7,6},{8,9},{9,8},{10,11... | collective-permute-start | bytes 983048 | tf_op jit(solution)/shard_map/ppermute | solution.py:244
  43.2 1.4 collective-permute-done.8
  44.6 1.8 add.107
  46.3 11.4 %all-to-all-start = ((f32[16,40,128]{2,1,0:T(8,128)}), f32[16,40,128]{2,1,0:T(8,128)S(1)}, u32[]{:S(2)}, u32[]{:S(2)}) async-start(f32[16,40,128]{2,1,0:T(8,128)} %bitcast.5), calls=%async_computation | async-start | bytes 655360 | tf_op jit(solution)/shard_map/all_to_all | solution.py:235
  58.9 1.5 pad_add_fusion.1
  60.4 5.0 %all-to-all-done = f32[16,40,128]{2,1,0:T(8,128)S(1)} async-done(((f32[16,40,128]{2,1,0:T(8,128)}), f32[16,40,128]{2,1,0:T(8,128)S(1)}, u32[]{:S(2)}, u32[]{:S(2)}) %all-to-all-start) | async-done | bytes 327712 | tf_op jit(solution)/shard_map/all_to_all | solution.py:235
  66.1 7.3 %all-to-all-start.1 = ((f32[8,40,128]{2,1,0:T(8,128)}), f32[8,40,128]{2,1,0:T(8,128)S(1)}, u32[]{:S(2)}, u32[]{:S(2)}) async-start(f32[8,40,128]{2,1,0:T(8,128)} %broadcast_in_dim.22), calls=%async_computation.1 | async-start | bytes 327680 | tf_op jit(solution)/shard_map/all_to_all | solution.py:235
  73.4 2.0 %slice_select_fusion.1 = (f32[2,128,384]{2,1,0:T(8,128)}, f32[2,128,384]{2,1,0:T(8,128)}) fusion(f32[2,384,384]{2,1,0:T(8,128)} %pad_add_fusion.1, pred[]{:T(512)S(6)} %eq.23), kind=kLoop, calls=%fused_computation.14 | loop fusion | flops 196608 | bytes 1572865 | tf_op jit(solution)/shard_map/jit(_where)/select_n | solution.py:211
  76.2 8.9 %collective-permute-start.7 = (f32[2,128,384]{2,1,0:T(8,128)}, f32[2,128,384]{2,1,0:T(8,128)}, u32[]{:S(2)}, u32[]{:S(2)}) collective-permute-start(f32[2,128,384]{2,1,0:T(8,128)} %get-tuple-element.21), channel_id=1, source_target_pairs={{32,64},{96,128},{160,192},{64,32},{128,96},{192,160},{33,65},{97,... | collective-permute-start | bytes 1179656 | tf_op jit(solution)/shard_map/ppermute | solution.py:208
  85.9 5.5 %all-to-all-start.2 = ((f32[16,40,128]{2,1,0:T(8,128)}), f32[16,40,128]{2,1,0:T(8,128)S(1)}, u32[]{:S(2)}, u32[]{:S(2)}) async-start(f32[16,40,128]{2,1,0:T(8,128)} %broadcast_in_dim.23), calls=%async_computation.2 | async-start | bytes 655360 | tf_op jit(solution)/shard_map/all_to_all | solution.py:235
  92.3 2.8 %collective-permute-done.7 = f32[2,128,384]{2,1,0:T(8,128)} collective-permute-done((f32[2,128,384]{2,1,0:T(8,128)}, f32[2,128,384]{2,1,0:T(8,128)}, u32[]{:S(2)}, u32[]{:S(2)}) %collective-permute-start.7) | collective-permute-done | bytes 393248 | tf_op jit(solution)/shard_map/ppermute | solution.py:208
  95.1 1.9 %broadcast_select_fusion.3 = (f32[2,128,384]{2,1,0:T(8,128)}, f32[2,128,384]{2,1,0:T(8,128)}) fusion(f32[2,128,384]{2,1,0:T(8,128)S(1)} %collective-permute-done.6, f32[2,128,384]{2,1,0:T(8,128)} %collective-permute-done.7, pred[]{:T(512)S(6)} %eq.23), kind=kLoop, calls=%fused_computation.24 | loop fusion | flops 196608 | bytes 1572865 | tf_op jit(solution)/shard_map/jit(_where)/select_n | solution.py:212
  97.0 1.2 all-to-all-done.2
  98.3 1.4 pad_add_fusion
  99.9 1.7 select_add_fusion.refs_3_
  101.6 11.3 %shard_map.114 = (f32[2,384,512]{2,1,0:T(8,128)S(1)}, f32[640,128]{1,0:T(8,128)S(1)}, f32[640,128]{1,0:T(8,128)S(1)}, f32[2,4,128,128]{3,2,1,0:T(8,128)S(1)}) custom-call(s32[8,2]{1,0:T(8,128)S(1)} %copy.14.refs_0_, s32[1]{0:T(128)} %bitcast.15.refs_1_, s32[1]{0:T(128)} %bitcast.2.refs_2_, f32[2,384,512]{2,1,0:T(8,128)} %select_add_fusion.refs_3_, ...), custom_call_target="tpu_custom_call" | custom-call | flops 6442450944 | bytes 6291456 | tf_op jit(solution)/shard_map/pallas_call | solution.py:191
  113.5 1.3 collective-permute-done.14
  115.5 5.9 %all-to-all-start.3 = ((f32[16,40,128]{2,1,0:T(8,128)}), f32[16,40,128]{2,1,0:T(8,128)S(1)}, u32[]{:S(2)}, u32[]{:S(2)}) async-start(f32[16,40,128]{2,1,0:T(8,128)} %bitcast.7), calls=%async_computation.3 | async-start | bytes 655360 | tf_op jit(solution)/shard_map/all_to_all | solution.py:235
  122.3 1.4 collective-permute-start.11
  123.8 5.4 %all-to-all-done.3 = f32[16,40,128]{2,1,0:T(8,128)S(1)} async-done(((f32[16,40,128]{2,1,0:T(8,128)}), f32[16,40,128]{2,1,0:T(8,128)S(1)}, u32[]{:S(2)}, u32[]{:S(2)}) %all-to-all-start.3) | async-done | bytes 327712 | tf_op jit(solution)/shard_map/all_to_all | solution.py:235
  129.8 12.5 %all-to-all-start.4 = ((f32[8,40,128]{2,1,0:T(8,128)}), f32[8,40,128]{2,1,0:T(8,128)S(1)}, u32[]{:S(2)}, u32[]{:S(2)}) async-start(f32[8,40,128]{2,1,0:T(8,128)} %broadcast_in_dim.40), calls=%async_computation.4 | async-start | bytes 327680 | tf_op jit(solution)/shard_map/all_to_all | solution.py:235
  143.6 8.2 %all-to-all-done.4 = f32[8,40,128]{2,1,0:T(8,128)S(1)} async-done(((f32[8,40,128]{2,1,0:T(8,128)}), f32[8,40,128]{2,1,0:T(8,128)S(1)}, u32[]{:S(2)}, u32[]{:S(2)}) %all-to-all-start.4) | async-done | bytes 163872 | tf_op jit(solution)/shard_map/all_to_all | solution.py:235
  152.5 6.1 %all-to-all-start.5 = ((f32[16,40,128]{2,1,0:T(8,128)}), f32[16,40,128]{2,1,0:T(8,128)S(1)}, u32[]{:S(2)}, u32[]{:S(2)}) async-start(f32[16,40,128]{2,1,0:T(8,128)} %broadcast_in_dim.41), calls=%async_computation.5 | async-start | bytes 655360 | tf_op jit(solution)/shard_map/all_to_all | solution.py:235
  159.6 3.0 %collective-permute-start.13 = (f32[2,64,256]{2,1,0:T(8,128)S(1)}, f32[2,64,256]{2,1,0:T(8,128)S(1)}, u32[]{:S(2)}, u32[]{:S(2)}) collective-permute-start(f32[2,64,256]{2,1,0:T(8,128)S(1)} %get-tuple-element.23), channel_id=1, source_target_pairs={{32,64},{96,128},{160,192},{64,32},{128,96},{192,160},{33,65},{97,... | collective-permute-start | bytes 393224 | tf_op jit(solution)/shard_map/ppermute | solution.py:208
  162.6 2.8 %all-to-all-done.5 = f32[16,40,128]{2,1,0:T(8,128)S(1)} async-done(((f32[16,40,128]{2,1,0:T(8,128)}), f32[16,40,128]{2,1,0:T(8,128)S(1)}, u32[]{:S(2)}, u32[]{:S(2)}) %all-to-all-start.5) | async-done | bytes 327712 | tf_op jit(solution)/shard_map/all_to_all | solution.py:235
  165.5 7.0 %collective-permute-done.13 = f32[2,64,256]{2,1,0:T(8,128)S(1)} collective-permute-done((f32[2,64,256]{2,1,0:T(8,128)S(1)}, f32[2,64,256]{2,1,0:T(8,128)S(1)}, u32[]{:S(2)}, u32[]{:S(2)}) %collective-permute-start.13) | collective-permute-done | bytes 131104 | tf_op jit(solution)/shard_map/ppermute | solution.py:208
  172.5 1.9 %fusion.1 = f32[2,256,256]{2,1,0:T(8,128)} fusion(f32[2,384,256]{2,1,0:T(8,128)S(1)} %pad_add_fusion.2, f32[2,384,512]{2,1,0:T(8,128)} %select_add_fusion.refs_3_, f32[2,64,256]{2,1,0:T(8,128)S(1)} %get-tuple-element.39, f32[2,64,256]{2,1,0:T(8,128)S(1)} %get-tuple-element.38), kind=kLoop, calls=%fused_computation.10 | loop fusion | flops 393216 | bytes 1835008 | tf_op jit(solution)/shard_map/add | solution.py:308
  (100 shorter events, 18.4 us)
Async XLA Ops:
  1.6 10.6 %collective-permute-start = (f32[2,64,256]{2,1,0:T(8,128)S(1)}, f32[2,64,256]{2,1,0:T(8,128)S(1)}, u32[]{:S(2)}, u32[]{:S(2)}) collective-permute-start(f32[2,64,256]{2,1,0:T(8,128)S(1)} %get-tuple-element.36), channel_id=1, source_target_pairs={{0,32},{64,96},{128,160},{192,224},{32,0},{96,64},{160,128},{224,1... | collective-permute-start | bytes 393224 | tf_op jit(solution)/shard_map/ppermute | solution.py:208
  2.6 13.0 %collective-permute-start.1 = (f32[2,64,256]{2,1,0:T(8,128)S(1)}, f32[2,64,256]{2,1,0:T(8,128)S(1)}, u32[]{:S(2)}, u32[]{:S(2)}) collective-permute-start(f32[2,64,256]{2,1,0:T(8,128)S(1)} %get-tuple-element.37), channel_id=1, source_target_pairs={{32,64},{96,128},{160,192},{64,32},{128,96},{192,160},{33,65},{97,... | collective-permute-start | bytes 393224 | tf_op jit(solution)/shard_map/ppermute | solution.py:208
  15.6 3.3 %copy-start.16 = (f32[2,64,256]{2,1,0:T(8,128)}, f32[2,64,256]{2,1,0:T(8,128)S(1)}, u32[]{:S(2)}) copy-start(f32[2,64,256]{2,1,0:T(8,128)S(1)} %get-tuple-element.40) | copy-start | bytes 393220
  15.6 3.3 %copy-start.18 = (f32[2,64,256]{2,1,0:T(8,128)}, f32[2,64,256]{2,1,0:T(8,128)S(1)}, u32[]{:S(2)}) copy-start(f32[2,64,256]{2,1,0:T(8,128)S(1)} %get-tuple-element.41) | copy-start | bytes 393220
  15.6 2.2 %copy-start.23 = (s32[1,1,8,2]{2,3,1,0:T(2,128)S(1)}, s32[1,1,8,2]{2,3,1,0:T(2,128)}, u32[]{:S(2)}) copy-start(s32[1,1,8,2]{2,3,1,0:T(2,128)} %param.14) | copy-start | bytes 196
  15.6 3.0 %copy-start.21 = (bf16[1,1,8,128,128]{4,3,2,1,0:T(8,128)(2,1)S(1)}, bf16[1,1,8,128,128]{4,3,2,1,0:T(8,128)(2,1)}, u32[]{:S(2)}) copy-start(bf16[1,1,8,128,128]{4,3,2,1,0:T(8,128)(2,1)} %param.12) | copy-start | bytes 786436
  15.6 3.0 %copy-start.22 = (f32[1,1,8,128]{3,2,1,0:T(8,128)S(1)}, f32[1,1,8,128]{3,2,1,0:T(8,128)}, u32[]{:S(2)}) copy-start(f32[1,1,8,128]{3,2,1,0:T(8,128)} %param.13) | copy-start | bytes 12292
  16.9 2.0 %copy-start.10 = (f32[2,256,256]{2,1,0:T(8,128)S(1)}, f32[2,256,256]{2,1,0:T(8,128)}, u32[]{:S(2)}) copy-start(f32[2,256,256]{2,1,0:T(8,128)} %param.10) | copy-start | bytes 1572868
  16.9 1.9 %collective-permute-start.2 = (f32[2,384,128]{2,1,0:T(8,128)S(1)}, f32[2,384,128]{2,1,0:T(8,128)S(1)}, u32[]{:S(2)}, u32[]{:S(2)}) collective-permute-start(f32[2,384,128]{2,1,0:T(8,128)S(1)} %get-tuple-element.32), channel_id=1, source_target_pairs={{0,1},{2,3},{4,5},{6,7},{8,9},{10,11},{12,13},{14,15},{16,17},{18,... | collective-permute-start | bytes 1179656 | tf_op jit(solution)/shard_map/ppermute | solution.py:208
  17.0 1.8 %collective-permute-start.3 = (f32[2,384,128]{2,1,0:T(8,128)S(1)}, f32[2,384,128]{2,1,0:T(8,128)S(1)}, u32[]{:S(2)}, u32[]{:S(2)}) collective-permute-start(f32[2,384,128]{2,1,0:T(8,128)S(1)} %get-tuple-element.33), channel_id=1, source_target_pairs={{1,2},{3,4},{5,6},{7,8},{9,10},{11,12},{13,14},{15,16},{17,18},{19... | collective-permute-start | bytes 1179656 | tf_op jit(solution)/shard_map/ppermute | solution.py:208
  31.7 26.0 %collective-permute-start.4 = (f32[2,384,128]{2,1,0:T(8,128)}, f32[2,384,128]{2,1,0:T(8,128)}, u32[]{:S(2)}, u32[]{:S(2)}) collective-permute-start(f32[2,384,128]{2,1,0:T(8,128)} %get-tuple-element.18), channel_id=1, source_target_pairs={{0,1},{2,3},{4,5},{6,7},{8,9},{10,11},{12,13},{14,15},{16,17},{18,... | collective-permute-start | bytes 1179656 | tf_op jit(solution)/shard_map/ppermute | solution.py:208
  39.5 18.3 %collective-permute-start.5 = (f32[2,384,128]{2,1,0:T(8,128)}, f32[2,384,128]{2,1,0:T(8,128)}, u32[]{:S(2)}, u32[]{:S(2)}) collective-permute-start(f32[2,384,128]{2,1,0:T(8,128)} %get-tuple-element.19), channel_id=1, source_target_pairs={{1,2},{3,4},{5,6},{7,8},{9,10},{11,12},{13,14},{15,16},{17,18},{19... | collective-permute-start | bytes 1179656 | tf_op jit(solution)/shard_map/ppermute | solution.py:208
  40.9 3.7 %collective-permute-start.8 = (f32[640,128]{1,0:T(8,128)S(1)}, f32[640,128]{1,0:T(8,128)}, u32[]{:S(2)}, u32[]{:S(2)}) collective-permute-start(f32[640,128]{1,0:T(8,128)S(1)} %get-tuple-element.11), channel_id=1, source_target_pairs={{0,1},{1,0},{2,3},{3,2},{4,5},{5,4},{6,7},{7,6},{8,9},{9,8},{10,11... | collective-permute-start | bytes 983048 | tf_op jit(solution)/shard_map/ppermute | solution.py:244
  46.3 19.1 %all-to-all-start = ((f32[16,40,128]{2,1,0:T(8,128)}), f32[16,40,128]{2,1,0:T(8,128)S(1)}, u32[]{:S(2)}, u32[]{:S(2)}) async-start(f32[16,40,128]{2,1,0:T(8,128)} %bitcast.5), calls=%async_computation | async-start | bytes 655360 | tf_op jit(solution)/shard_map/all_to_all | solution.py:235
  66.1 19.0 %all-to-all-start.1 = ((f32[8,40,128]{2,1,0:T(8,128)}), f32[8,40,128]{2,1,0:T(8,128)S(1)}, u32[]{:S(2)}, u32[]{:S(2)}) async-start(f32[8,40,128]{2,1,0:T(8,128)} %broadcast_in_dim.22), calls=%async_computation.1 | async-start | bytes 327680 | tf_op jit(solution)/shard_map/all_to_all | solution.py:235
  75.5 22.8 %copy-start.9 = (f32[2,384,384]{2,1,0:T(8,128)S(1)}, f32[2,384,384]{2,1,0:T(8,128)}, u32[]{:S(2)}) copy-start(f32[2,384,384]{2,1,0:T(8,128)} %pad_add_fusion.1) | copy-start | bytes 3538948
  75.5 16.8 %collective-permute-start.6 = (f32[2,128,384]{2,1,0:T(8,128)}, f32[2,128,384]{2,1,0:T(8,128)S(1)}, u32[]{:S(2)}, u32[]{:S(2)}) collective-permute-start(f32[2,128,384]{2,1,0:T(8,128)} %get-tuple-element.20), channel_id=1, source_target_pairs={{0,32},{64,96},{128,160},{192,224},{32,0},{96,64},{160,128},{224,1... | collective-permute-start | bytes 1179656 | tf_op jit(solution)/shard_map/ppermute | solution.py:208
  76.2 18.9 %collective-permute-start.7 = (f32[2,128,384]{2,1,0:T(8,128)}, f32[2,128,384]{2,1,0:T(8,128)}, u32[]{:S(2)}, u32[]{:S(2)}) collective-permute-start(f32[2,128,384]{2,1,0:T(8,128)} %get-tuple-element.21), channel_id=1, source_target_pairs={{32,64},{96,128},{160,192},{64,32},{128,96},{192,160},{33,65},{97,... | collective-permute-start | bytes 1179656 | tf_op jit(solution)/shard_map/ppermute | solution.py:208
  85.9 12.3 %all-to-all-start.2 = ((f32[16,40,128]{2,1,0:T(8,128)}), f32[16,40,128]{2,1,0:T(8,128)S(1)}, u32[]{:S(2)}, u32[]{:S(2)}) async-start(f32[16,40,128]{2,1,0:T(8,128)} %broadcast_in_dim.23), calls=%async_computation.2 | async-start | bytes 655360 | tf_op jit(solution)/shard_map/all_to_all | solution.py:235
  98.3 3.3 %collective-permute-start.9 = (f32[640,128]{1,0:T(8,128)S(1)}, f32[640,128]{1,0:T(8,128)S(1)}, u32[]{:S(2)}, u32[]{:S(2)}) collective-permute-start(f32[640,128]{1,0:T(8,128)S(1)} %bitcast.16), channel_id=1, source_target_pairs={{0,1},{1,0},{2,3},{3,2},{4,5},{5,4},{6,7},{7,6},{8,9},{9,8},{10,11... | collective-permute-start | bytes 983048 | tf_op jit(solution)/shard_map/ppermute | solution.py:244
  99.9 1.7 copy-start.4
  99.9 1.7 copy-start.6
  99.9 1.7 copy-start.8
  112.9 1.8 %collective-permute-start.14 = (f32[640,128]{1,0:T(8,128)S(1)}, f32[640,128]{1,0:T(8,128)S(1)}, u32[]{:S(2)}, u32[]{:S(2)}) collective-permute-start(f32[640,128]{1,0:T(8,128)S(1)} %get-tuple-element.15), channel_id=1, source_target_pairs={{0,1},{1,0},{2,3},{3,2},{4,5},{5,4},{6,7},{7,6},{8,9},{9,8},{10,11... | collective-permute-start | bytes 983048 | tf_op jit(solution)/shard_map/ppermute | solution.py:244
  115.5 13.6 %all-to-all-start.3 = ((f32[16,40,128]{2,1,0:T(8,128)}), f32[16,40,128]{2,1,0:T(8,128)S(1)}, u32[]{:S(2)}, u32[]{:S(2)}) async-start(f32[16,40,128]{2,1,0:T(8,128)} %bitcast.7), calls=%async_computation.3 | async-start | bytes 655360 | tf_op jit(solution)/shard_map/all_to_all | solution.py:235
  122.3 20.0 %collective-permute-start.10 = (f32[2,384,64]{2,1,0:T(8,128)}, f32[2,384,64]{2,1,0:T(8,128)S(1)}, u32[]{:S(2)}, u32[]{:S(2)}) collective-permute-start(f32[2,384,64]{2,1,0:T(8,128)} %get-tuple-element.16), channel_id=1, source_target_pairs={{0,1},{2,3},{4,5},{6,7},{8,9},{10,11},{12,13},{14,15},{16,17},{18,... | collective-permute-start | bytes 589832 | tf_op jit(solution)/shard_map/ppermute | solution.py:208
  122.3 20.0 %collective-permute-start.11 = (f32[2,384,64]{2,1,0:T(8,128)S(1)}, f32[2,384,64]{2,1,0:T(8,128)}, u32[]{:S(2)}, u32[]{:S(2)}) collective-permute-start(f32[2,384,64]{2,1,0:T(8,128)S(1)} %get-tuple-element.17), channel_id=1, source_target_pairs={{1,2},{3,4},{5,6},{7,8},{9,10},{11,12},{13,14},{15,16},{17,18},{19... | collective-permute-start | bytes 589832 | tf_op jit(solution)/shard_map/ppermute | solution.py:208
  129.8 21.9 %all-to-all-start.4 = ((f32[8,40,128]{2,1,0:T(8,128)}), f32[8,40,128]{2,1,0:T(8,128)S(1)}, u32[]{:S(2)}, u32[]{:S(2)}) async-start(f32[8,40,128]{2,1,0:T(8,128)} %broadcast_in_dim.40), calls=%async_computation.4 | async-start | bytes 327680 | tf_op jit(solution)/shard_map/all_to_all | solution.py:235
  152.5 13.0 %all-to-all-start.5 = ((f32[16,40,128]{2,1,0:T(8,128)}), f32[16,40,128]{2,1,0:T(8,128)S(1)}, u32[]{:S(2)}, u32[]{:S(2)}) async-start(f32[16,40,128]{2,1,0:T(8,128)} %broadcast_in_dim.41), calls=%async_computation.5 | async-start | bytes 655360 | tf_op jit(solution)/shard_map/all_to_all | solution.py:235
  158.7 6.8 %collective-permute-start.12 = (f32[2,64,256]{2,1,0:T(8,128)S(1)}, f32[2,64,256]{2,1,0:T(8,128)S(1)}, u32[]{:S(2)}, u32[]{:S(2)}) collective-permute-start(f32[2,64,256]{2,1,0:T(8,128)S(1)} %get-tuple-element.22), channel_id=1, source_target_pairs={{0,32},{64,96},{128,160},{192,224},{32,0},{96,64},{160,128},{224,1... | collective-permute-start | bytes 393224 | tf_op jit(solution)/shard_map/ppermute | solution.py:208
  159.6 12.9 %collective-permute-start.13 = (f32[2,64,256]{2,1,0:T(8,128)S(1)}, f32[2,64,256]{2,1,0:T(8,128)S(1)}, u32[]{:S(2)}, u32[]{:S(2)}) collective-permute-start(f32[2,64,256]{2,1,0:T(8,128)S(1)} %get-tuple-element.23), channel_id=1, source_target_pairs={{32,64},{96,128},{160,192},{64,32},{128,96},{192,160},{33,65},{97,... | collective-permute-start | bytes 393224 | tf_op jit(solution)/shard_map/ppermute | solution.py:208
  165.5 8.9 %collective-permute-start.15 = (f32[640,128]{1,0:T(8,128)S(1)}, f32[640,128]{1,0:T(8,128)S(1)}, u32[]{:S(2)}, u32[]{:S(2)}) collective-permute-start(f32[640,128]{1,0:T(8,128)S(1)} %bitcast.19), channel_id=1, source_target_pairs={{0,1},{1,0},{2,3},{3,2},{4,5},{5,4},{6,7},{7,6},{8,9},{9,8},{10,11... | collective-permute-start | bytes 983048 | tf_op jit(solution)/shard_map/ppermute | solution.py:244
  (14 other events, 19.1 us)
where the time goes:
time: 177 us; the launch traced here: 175 us
  starting transfers between devices  87.3 us (49%)
  waiting for transfers between devices  38.3 us (22%)
  other arithmetic  22.1 us (12%)
  Pallas kernels  21.5 us (12%)
  local copies, waits for them, and re-layouts  4.4 us (2%)
  between operations  1.8 us (1%)
    all_to_all x6, starting transfers between devices, exchange(): lax.all_to_all(blocks, AXES, 0, 0, axis_index_groups=members, tiled=True)  48.8 us
    ppermute x12, starting transfers between devices, meet(): return lax.ppermute(block, axis, pairs + [(j, i) for i, j in pairs])  35.7 us
    all_to_all x6, waiting for transfers between devices, exchange(): lax.all_to_all(blocks, AXES, 0, 0, axis_index_groups=members, tiled=True)  22.6 us
    pallas_call x2, Pallas kernels, run_pass(): pl.pallas_call(functools.partial(pass_kernel, modes=modes, size=size, mar...  21.5 us
    ppermute x12, waiting for transfers between devices, meet(): return lax.ppermute(block, axis, pairs + [(j, i) for i, j in pairs])  13.1 us
    select_n x6, other arithmetic, neighbours(): second = meet(jnp.where(odd, low_strip, high_strip), 0)  5.18 us
    select_n x6, other arithmetic, neighbours(): return (jnp.where(odd, second, first), jnp.where(odd, first, second))  4.25 us
  transfers between devices with their start and end apart: 22, of which 10 were waited for; matrix products, arithmetic and copies ran while one was open for 10% of the time, Pallas kernels for 0%

commit v1 on v0

--- a/solution.py
+++ b/solution.py
@@ -284,27 +284,30 @@
     inside = inside & (at_col >= 0) & (at_col < cols * lax.axis_size("col"))
     core = (lax.axis_index("col") % CORES).reshape(1)
     left, right = margin, LANES + cols + rim
+
+    def folded(updates):
+        strips = at(updates, 2, left, right)
+        low, high = neighbours(at(strips, 1, 0, rim), at(strips, 1, tall - rim, tall), "row")
+        middle = at(strips, 1, rim, rim + rows)
+        return middle + padded(low, 1, 0, rows) + padded(high, 1, rows - rim, rows)
+
     updates, mine, other = run_pass(starts, count, core, frame, probe, None, amplitude, tables, margin)
     means = total(mine, other)
-    strips = at(updates, 2, left, right)
-    low, high = neighbours(at(strips, 2, 0, 2 * rim), at(strips, 2, cols, cols + 2 * rim), "col")
-    strips = strips + padded(low, 2, 0, cols + 2 * rim) + padded(high, 2, cols, cols + 2 * rim)
-    low, high = neighbours(at(strips, 1, 0, 2 * rim), at(strips, 1, rows, tall), "row")
-    strips = strips + padded(low, 1, 0, tall) + padded(high, 1, rows, tall)
-    updates = padded(strips, 2, left, wide)
-    frame = frame + jnp.where(inside, updates, 0.0)
+    middle = folded(updates)
+    low, high = neighbours(at(middle, 2, 0, 2 * rim), at(middle, 2, cols, cols + 2 * rim), "col")
+    middle = middle + padded(low, 2, 0, cols + 2 * rim) + padded(high, 2, cols, cols + 2 * rim)
+    low, high = neighbours(at(middle, 1, 0, rim), at(middle, 1, rows - rim, rows), "row")
+    whole = jnp.concatenate([low, middle, high], axis=1)
+    frame = frame + jnp.where(inside, padded(whole, 2, left, wide), 0.0)
 
     updates, mine, other, probe = run_pass(
         starts, count, core, frame, probe, means, amplitude, tables, margin
     )
     mine, other = total(mine, other)
-    strips = at(updates, 2, left, right)
-    low, high = neighbours(at(strips, 2, 0, rim), at(strips, 2, rim + cols, cols + 2 * rim), "col")
-    middle = at(strips, 2, rim, rim + cols)
-    middle = middle + padded(low, 2, 0, cols) + padded(high, 2, cols - rim, cols)
-    low, high = neighbours(at(middle, 1, 0, rim), at(middle, 1, tall - rim, tall), "row")
-    tile = at(middle, 1, rim, rim + rows)
-    tile = tile + padded(low, 1, 0, rows) + padded(high, 1, rows - rim, rows)
+    middle = folded(updates)
+    low, high = neighbours(at(middle, 2, 0, rim), at(middle, 2, rim + cols, cols + 2 * rim), "col")
+    tile = at(middle, 2, rim, rim + cols)
+    tile = tile + padded(low, 2, 0, cols) + padded(high, 2, cols - rim, cols)
     object_out = frame[:, rim : rim + rows, LANES : LANES + cols] + tile
     lower = jnp.where(core[0] == 0, mine, other)
     upper = jnp.where(core[0] == 0, other, mine)

time: 177 us -> 179 us (1.011)
  the two profiles are of different devices: /device:TPU:6 before, /device:TPU:63 now
where the time goes in v1:
time: 179 us; the launch traced here: 176 us
  starting transfers between devices  91.5 us (51%)
  waiting for transfers between devices  37 us (21%)
  Pallas kernels  21 us (12%)
  other arithmetic  19.5 us (11%)
  local copies, waits for them, and re-layouts  5 us (3%)
  between operations  1.85 us (1%)
    ppermute x14, starting transfers between devices, meet(): return lax.ppermute(block, axis, pairs + [(j, i) for i, j in pairs])  46.1 us
    all_to_all x6, starting transfers between devices, exchange(): lax.all_to_all(blocks, AXES, 0, 0, axis_index_groups=members, tiled=True)  39.5 us
    ppermute x14, waiting for transfers between devices, meet(): return lax.ppermute(block, axis, pairs + [(j, i) for i, j in pairs])  33.1 us
    pallas_call x2, Pallas kernels, run_pass(): pl.pallas_call(functools.partial(pass_kernel, modes=modes, size=size, mar...  21 us
    ppermute x4, starting transfers between devices, swap(): return lax.ppermute(block, 'col', [(i, i ^ 1) for i in range(count)])  5.97 us
    select_n x7, other arithmetic, neighbours(): return (jnp.where(odd, second, first), jnp.where(odd, first, second))  3.74 us
  transfers between devices with their start and end apart: 24, of which 9 were waited for; matrix products, arithmetic and copies ran while one was open for 9% of the time, Pallas kernels for 0%

profile of v1, /device:TPU:63, one launch (start us, length us, event | category | flops | bytes accessed | tf_op | source)
XLA Modules:
  0.0 175.9 jit_solution(11407842844083534139)
XLA Ops:
  2.3 8.5 %collective-permute-start.1 = (f32[2,64,256]{2,1,0:T(8,128)S(1)}, f32[2,64,256]{2,1,0:T(8,128)S(1)}, u32[]{:S(2)}, u32[]{:S(2)}) collective-permute-start(f32[2,64,256]{2,1,0:T(8,128)S(1)} %get-tuple-element.37), channel_id=1, source_target_pairs={{32,64},{96,128},{160,192},{64,32},{128,96},{192,160},{33,65},{97,... | collective-permute-start | bytes 393224 | tf_op jit(solution)/shard_map/ppermute | solution.py:208
  10.8 4.9 %collective-permute-done.1 = f32[2,64,256]{2,1,0:T(8,128)S(1)} collective-permute-done((f32[2,64,256]{2,1,0:T(8,128)S(1)}, f32[2,64,256]{2,1,0:T(8,128)S(1)}, u32[]{:S(2)}, u32[]{:S(2)}) %collective-permute-start.1) | collective-permute-done | bytes 131104 | tf_op jit(solution)/shard_map/ppermute | solution.py:208
  17.1 3.3 %collective-permute-start.2 = (f32[2,384,128]{2,1,0:T(8,128)S(1)}, f32[2,384,128]{2,1,0:T(8,128)S(1)}, u32[]{:S(2)}, u32[]{:S(2)}) collective-permute-start(f32[2,384,128]{2,1,0:T(8,128)S(1)} %get-tuple-element.28), channel_id=1, source_target_pairs={{0,1},{2,3},{4,5},{6,7},{8,9},{10,11},{12,13},{14,15},{16,17},{18,... | collective-permute-start | bytes 1179656 | tf_op jit(solution)/shard_map/ppermute | solution.py:208
  20.4 2.3 %collective-permute-start.3 = (f32[2,384,128]{2,1,0:T(8,128)S(1)}, f32[2,384,128]{2,1,0:T(8,128)S(1)}, u32[]{:S(2)}, u32[]{:S(2)}) collective-permute-start(f32[2,384,128]{2,1,0:T(8,128)S(1)} %get-tuple-element.29), channel_id=1, source_target_pairs={{1,2},{3,4},{5,6},{7,8},{9,10},{11,12},{13,14},{15,16},{17,18},{19... | collective-permute-start | bytes 1179656 | tf_op jit(solution)/shard_map/ppermute | solution.py:208
  23.7 7.9 %collective-permute-done.3 = f32[2,384,128]{2,1,0:T(8,128)S(1)} collective-permute-done((f32[2,384,128]{2,1,0:T(8,128)S(1)}, f32[2,384,128]{2,1,0:T(8,128)S(1)}, u32[]{:S(2)}, u32[]{:S(2)}) %collective-permute-start.3) | collective-permute-done | bytes 393248 | tf_op jit(solution)/shard_map/ppermute | solution.py:208
  33.0 10.2 %shard_map.113 = (f32[2,384,512]{2,1,0:T(8,128)S(1)}, f32[640,128]{1,0:T(8,128)S(1)}, f32[640,128]{1,0:T(8,128)S(1)}) custom-call(s32[8,2]{1,0:T(8,128)S(1)} %copy.14.refs_0_, s32[1]{0:T(128)} %bitcast.14.refs_1_, s32[1]{0:T(128)} %bitcast.2.refs_2_, f32[2,384,512]{2,1,0:T(8,128)S(1)} %pad_maximum_fusion.refs_3_, f32[2,4,128,128]{3,2,1,0:T(8,128)S(1)} %copy-done, ...), custom_call_target="tpu_custom_call" | custom-call | flops 6442450944 | bytes 6291456 | tf_op jit(solution)/shard_map/pallas_call | solution.py:191
  43.4 8.5 %collective-permute-start.5 = (f32[2,64,384]{2,1,0:T(8,128)S(1)}, f32[2,64,384]{2,1,0:T(8,128)S(1)}, u32[]{:S(2)}, u32[]{:S(2)}) collective-permute-start(f32[2,64,384]{2,1,0:T(8,128)S(1)} %get-tuple-element.19), channel_id=1, source_target_pairs={{32,64},{96,128},{160,192},{64,32},{128,96},{192,160},{33,65},{97,... | collective-permute-start | bytes 589832 | tf_op jit(solution)/shard_map/ppermute | solution.py:208
  52.0 5.4 %collective-permute-done.5 = f32[2,64,384]{2,1,0:T(8,128)S(1)} collective-permute-done((f32[2,64,384]{2,1,0:T(8,128)S(1)}, f32[2,64,384]{2,1,0:T(8,128)S(1)}, u32[]{:S(2)}, u32[]{:S(2)}) %collective-permute-start.5) | collective-permute-done | bytes 196640 | tf_op jit(solution)/shard_map/ppermute | solution.py:208
  58.6 1.9 %collective-permute-start.7 = (f32[2,256,128]{2,1,0:T(8,128)}, f32[2,256,128]{2,1,0:T(8,128)}, u32[]{:S(2)}, u32[]{:S(2)}) collective-permute-start(f32[2,256,128]{2,1,0:T(8,128)} %get-tuple-element.25), channel_id=1, source_target_pairs={{1,2},{3,4},{5,6},{7,8},{9,10},{11,12},{13,14},{15,16},{17,18},{19... | collective-permute-start | bytes 786440 | tf_op jit(solution)/shard_map/ppermute | solution.py:208
  60.5 1.7 add.108
  62.3 8.2 %all-to-all-start = ((f32[16,40,128]{2,1,0:T(8,128)}), f32[16,40,128]{2,1,0:T(8,128)S(1)}, u32[]{:S(2)}, u32[]{:S(2)}) async-start(f32[16,40,128]{2,1,0:T(8,128)} %bitcast.5), calls=%async_computation | async-start | bytes 655360 | tf_op jit(solution)/shard_map/all_to_all | solution.py:235
  70.5 1.8 %broadcast_select_fusion.7 = (f32[2,256,128]{2,1,0:T(8,128)S(1)}, f32[2,256,128]{2,1,0:T(8,128)}) fusion(f32[2,256,128]{2,1,0:T(8,128)} %collective-permute-done.6, f32[2,256,128]{2,1,0:T(8,128)} %collective-permute-done.7, pred[]{:T(512)S(6)} %eq.24), kind=kLoop, calls=%fused_computation.38 | loop fusion | flops 131072 | bytes 1048577 | tf_op jit(solution)/shard_map/jit(_where)/select_n | solution.py:212
  72.2 2.2 %all-to-all-done = f32[16,40,128]{2,1,0:T(8,128)S(1)} async-done(((f32[16,40,128]{2,1,0:T(8,128)}), f32[16,40,128]{2,1,0:T(8,128)S(1)}, u32[]{:S(2)}, u32[]{:S(2)}) %all-to-all-start) | async-done | bytes 327712 | tf_op jit(solution)/shard_map/all_to_all | solution.py:235
  75.1 8.2 %all-to-all-start.1 = ((f32[8,40,128]{2,1,0:T(8,128)}), f32[8,40,128]{2,1,0:T(8,128)S(1)}, u32[]{:S(2)}, u32[]{:S(2)}) async-start(f32[8,40,128]{2,1,0:T(8,128)} %broadcast_in_dim.22), calls=%async_computation.1 | async-start | bytes 327680 | tf_op jit(solution)/shard_map/all_to_all | solution.py:235
  86.8 7.1 %collective-permute-start.9 = (f32[2,64,384]{2,1,0:T(8,128)}, f32[2,64,384]{2,1,0:T(8,128)}, u32[]{:S(2)}, u32[]{:S(2)}) collective-permute-start(f32[2,64,384]{2,1,0:T(8,128)} %get-tuple-element.23), channel_id=1, source_target_pairs={{32,64},{96,128},{160,192},{64,32},{128,96},{192,160},{33,65},{97,... | collective-permute-start | bytes 589832 | tf_op jit(solution)/shard_map/ppermute | solution.py:208
  94.7 6.7 %all-to-all-start.2 = ((f32[16,40,128]{2,1,0:T(8,128)}), f32[16,40,128]{2,1,0:T(8,128)S(1)}, u32[]{:S(2)}, u32[]{:S(2)}) async-start(f32[16,40,128]{2,1,0:T(8,128)} %broadcast_in_dim.23), calls=%async_computation.2 | async-start | bytes 655360 | tf_op jit(solution)/shard_map/all_to_all | solution.py:235
  102.2 2.0 %collective-permute-done.9 = f32[2,64,384]{2,1,0:T(8,128)} collective-permute-done((f32[2,64,384]{2,1,0:T(8,128)}, f32[2,64,384]{2,1,0:T(8,128)}, u32[]{:S(2)}, u32[]{:S(2)}) %collective-permute-start.9) | collective-permute-done | bytes 196640 | tf_op jit(solution)/shard_map/ppermute | solution.py:208
  104.2 1.8 %broadcast_select_fusion.11 = (f32[2,64,384]{2,1,0:T(8,128)}, f32[2,64,384]{2,1,0:T(8,128)}) fusion(f32[2,64,384]{2,1,0:T(8,128)} %collective-permute-done.8, f32[2,64,384]{2,1,0:T(8,128)} %collective-permute-done.9, pred[]{:T(512)S(6)} %eq.25), kind=kLoop, calls=%fused_computation.44 | loop fusion | flops 98304 | bytes 786433 | tf_op jit(solution)/shard_map/jit(_where)/select_n | solution.py:212
  106.1 3.8 %collective-permute-start.11 = (f32[640,128]{1,0:T(8,128)S(1)}, f32[640,128]{1,0:T(8,128)S(1)}, u32[]{:S(2)}, u32[]{:S(2)}) collective-permute-start(f32[640,128]{1,0:T(8,128)S(1)} %bitcast.16), channel_id=1, source_target_pairs={{0,1},{1,0},{2,3},{3,2},{4,5},{5,4},{6,7},{7,6},{8,9},{9,8},{10,11... | collective-permute-start | bytes 983048 | tf_op jit(solution)/shard_map/ppermute | solution.py:244
  110.0 3.0 %fusion.1.refs_3_ = f32[2,384,512]{2,1,0:T(8,128)} fusion(f32[2,64,384]{2,1,0:T(8,128)} %get-tuple-element.41, f32[2,256,384]{2,1,0:T(8,128)S(1)} %copy-done.11, f32[2,64,384]{2,1,0:T(8,128)} %get-tuple-element.40, pred[384,512]{1,0:T(8,128)(4,1)} %and_and_fusion, f32[2,384,128]{2,1,0:T(8,128)S(1)} %copy-done.13, f32[2,64,256]{2,1,0:T(8,128)} %copy-done.15, ...), kind=kLoop, calls=%fused_computation.4 | loop fusion | flops 5505024 | bytes 4521984 | tf_op jit(solution)/shard_map/add | solution.py:301
  113.0 10.8 %shard_map.114 = (f32[2,384,512]{2,1,0:T(8,128)S(1)}, f32[640,128]{1,0:T(8,128)S(1)}, f32[640,128]{1,0:T(8,128)S(1)}, f32[2,4,128,128]{3,2,1,0:T(8,128)S(1)}) custom-call(s32[8,2]{1,0:T(8,128)S(1)} %copy.14.refs_0_, s32[1]{0:T(128)} %bitcast.15.refs_1_, s32[1]{0:T(128)} %bitcast.2.refs_2_, f32[2,384,512]{2,1,0:T(8,128)} %fusion.1.refs_3_, ...), custom_call_target="tpu_custom_call" | custom-call | flops 6442450944 | bytes 6291456 | tf_op jit(solution)/shard_map/pallas_call | solution.py:191
  123.9 1.6 collective-permute-done.16
  126.2 6.1 %all-to-all-start.3 = ((f32[16,40,128]{2,1,0:T(8,128)}), f32[16,40,128]{2,1,0:T(8,128)S(1)}, u32[]{:S(2)}, u32[]{:S(2)}) async-start(f32[16,40,128]{2,1,0:T(8,128)} %bitcast.7), calls=%async_computation.3 | async-start | bytes 655360 | tf_op jit(solution)/shard_map/all_to_all | solution.py:235
  133.2 6.6 %collective-permute-start.13 = (f32[2,64,384]{2,1,0:T(8,128)S(1)}, f32[2,64,384]{2,1,0:T(8,128)S(1)}, u32[]{:S(2)}, u32[]{:S(2)}) collective-permute-start(f32[2,64,384]{2,1,0:T(8,128)S(1)} %get-tuple-element.17), channel_id=1, source_target_pairs={{32,64},{96,128},{160,192},{64,32},{128,96},{192,160},{33,65},{97,... | collective-permute-start | bytes 589832 | tf_op jit(solution)/shard_map/ppermute | solution.py:208
  140.5 3.9 %all-to-all-start.4 = ((f32[8,40,128]{2,1,0:T(8,128)}), f32[8,40,128]{2,1,0:T(8,128)S(1)}, u32[]{:S(2)}, u32[]{:S(2)}) async-start(f32[8,40,128]{2,1,0:T(8,128)} %broadcast_in_dim.40), calls=%async_computation.4 | async-start | bytes 327680 | tf_op jit(solution)/shard_map/all_to_all | solution.py:235
  144.4 7.8 %collective-permute-done.13 = f32[2,64,384]{2,1,0:T(8,128)S(1)} collective-permute-done((f32[2,64,384]{2,1,0:T(8,128)S(1)}, f32[2,64,384]{2,1,0:T(8,128)S(1)}, u32[]{:S(2)}, u32[]{:S(2)}) %collective-permute-start.13) | collective-permute-done | bytes 196640 | tf_op jit(solution)/shard_map/ppermute | solution.py:208
  153.3 6.4 %all-to-all-start.5 = ((f32[16,40,128]{2,1,0:T(8,128)}), f32[16,40,128]{2,1,0:T(8,128)S(1)}, u32[]{:S(2)}, u32[]{:S(2)}) async-start(f32[16,40,128]{2,1,0:T(8,128)} %broadcast_in_dim.41), calls=%async_computation.5 | async-start | bytes 655360 | tf_op jit(solution)/shard_map/all_to_all | solution.py:235
  159.8 3.1 %collective-permute-start.14 = (f32[2,256,64]{2,1,0:T(8,128)S(1)}, f32[2,256,64]{2,1,0:T(8,128)S(1)}, u32[]{:S(2)}, u32[]{:S(2)}) collective-permute-start(f32[2,256,64]{2,1,0:T(8,128)S(1)} %get-tuple-element.20), channel_id=1, source_target_pairs={{0,1},{2,3},{4,5},{6,7},{8,9},{10,11},{12,13},{14,15},{16,17},{18,... | collective-permute-start | bytes 393224 | tf_op jit(solution)/shard_map/ppermute | solution.py:208
  162.9 2.7 %collective-permute-start.15 = (f32[2,256,64]{2,1,0:T(8,128)S(1)}, f32[2,256,64]{2,1,0:T(8,128)S(1)}, u32[]{:S(2)}, u32[]{:S(2)}) collective-permute-start(f32[2,256,64]{2,1,0:T(8,128)S(1)} %get-tuple-element.21), channel_id=1, source_target_pairs={{1,2},{3,4},{5,6},{7,8},{9,10},{11,12},{13,14},{15,16},{17,18},{19... | collective-permute-start | bytes 393224 | tf_op jit(solution)/shard_map/ppermute | solution.py:208
  165.6 2.0 %collective-permute-start.17 = (f32[640,128]{1,0:T(8,128)S(1)}, f32[640,128]{1,0:T(8,128)S(1)}, u32[]{:S(2)}, u32[]{:S(2)}) collective-permute-start(f32[640,128]{1,0:T(8,128)S(1)} %bitcast.19), channel_id=1, source_target_pairs={{0,1},{1,0},{2,3},{3,2},{4,5},{5,4},{6,7},{7,6},{8,9},{9,8},{10,11... | collective-permute-start | bytes 983048 | tf_op jit(solution)/shard_map/ppermute | solution.py:244
  167.6 5.1 %collective-permute-done.15 = f32[2,256,64]{2,1,0:T(8,128)S(1)} collective-permute-done((f32[2,256,64]{2,1,0:T(8,128)S(1)}, f32[2,256,64]{2,1,0:T(8,128)S(1)}, u32[]{:S(2)}, u32[]{:S(2)}) %collective-permute-start.15) | collective-permute-done | bytes 131104 | tf_op jit(solution)/shard_map/ppermute | solution.py:208
  172.8 2.1 %fusion.4 = f32[2,256,256]{2,1,0:T(8,128)} fusion(f32[2,256,384]{2,1,0:T(8,128)S(1)} %pad_add_fusion, f32[2,384,512]{2,1,0:T(8,128)} %fusion.1.refs_3_, f32[2,256,64]{2,1,0:T(8,128)S(1)} %get-tuple-element.33, f32[2,256,64]{2,1,0:T(8,128)S(1)} %get-tuple-element.32), kind=kLoop, calls=%fused_computation.16 | loop fusion | flops 393216 | bytes 1835008 | tf_op jit(solution)/shard_map/add | solution.py:311
  (96 shorter events, 16.5 us)
Async XLA Ops:
  1.6 9.1 %collective-permute-start = (f32[2,64,256]{2,1,0:T(8,128)S(1)}, f32[2,64,256]{2,1,0:T(8,128)S(1)}, u32[]{:S(2)}, u32[]{:S(2)}) collective-permute-start(f32[2,64,256]{2,1,0:T(8,128)S(1)} %get-tuple-element.36), channel_id=1, source_target_pairs={{0,32},{64,96},{128,160},{192,224},{32,0},{96,64},{160,128},{224,1... | collective-permute-start | bytes 393224 | tf_op jit(solution)/shard_map/ppermute | solution.py:208
  2.3 13.4 %collective-permute-start.1 = (f32[2,64,256]{2,1,0:T(8,128)S(1)}, f32[2,64,256]{2,1,0:T(8,128)S(1)}, u32[]{:S(2)}, u32[]{:S(2)}) collective-permute-start(f32[2,64,256]{2,1,0:T(8,128)S(1)} %get-tuple-element.37), channel_id=1, source_target_pairs={{32,64},{96,128},{160,192},{64,32},{128,96},{192,160},{33,65},{97,... | collective-permute-start | bytes 393224 | tf_op jit(solution)/shard_map/ppermute | solution.py:208
  15.7 15.9 %copy-start.14 = (f32[2,64,256]{2,1,0:T(8,128)}, f32[2,64,256]{2,1,0:T(8,128)S(1)}, u32[]{:S(2)}) copy-start(f32[2,64,256]{2,1,0:T(8,128)S(1)} %get-tuple-element.44) | copy-start | bytes 393220
  15.8 15.9 %copy-start.15 = (f32[2,64,256]{2,1,0:T(8,128)}, f32[2,64,256]{2,1,0:T(8,128)S(1)}, u32[]{:S(2)}) copy-start(f32[2,64,256]{2,1,0:T(8,128)S(1)} %get-tuple-element.45) | copy-start | bytes 393220
  15.8 6.9 %copy-start.18 = (s32[1,1,8,2]{2,3,1,0:T(2,128)S(1)}, s32[1,1,8,2]{2,3,1,0:T(2,128)}, u32[]{:S(2)}) copy-start(s32[1,1,8,2]{2,3,1,0:T(2,128)} %param.14) | copy-start | bytes 196
  15.8 7.7 %copy-start.16 = (bf16[1,1,8,128,128]{4,3,2,1,0:T(8,128)(2,1)S(1)}, bf16[1,1,8,128,128]{4,3,2,1,0:T(8,128)(2,1)}, u32[]{:S(2)}) copy-start(bf16[1,1,8,128,128]{4,3,2,1,0:T(8,128)(2,1)} %param.12) | copy-start | bytes 786436
  15.8 7.7 %copy-start.17 = (f32[1,1,8,128]{3,2,1,0:T(8,128)S(1)}, f32[1,1,8,128]{3,2,1,0:T(8,128)}, u32[]{:S(2)}) copy-start(f32[1,1,8,128]{3,2,1,0:T(8,128)} %param.13) | copy-start | bytes 12292
  17.1 14.6 %copy-start.9 = (f32[2,256,256]{2,1,0:T(8,128)S(1)}, f32[2,256,256]{2,1,0:T(8,128)}, u32[]{:S(2)}) copy-start(f32[2,256,256]{2,1,0:T(8,128)} %param.10) | copy-start | bytes 1572868
  17.1 6.6 %collective-permute-start.2 = (f32[2,384,128]{2,1,0:T(8,128)S(1)}, f32[2,384,128]{2,1,0:T(8,128)S(1)}, u32[]{:S(2)}, u32[]{:S(2)}) collective-permute-start(f32[2,384,128]{2,1,0:T(8,128)S(1)} %get-tuple-element.28), channel_id=1, source_target_pairs={{0,1},{2,3},{4,5},{6,7},{8,9},{10,11},{12,13},{14,15},{16,17},{18,... | collective-permute-start | bytes 1179656 | tf_op jit(solution)/shard_map/ppermute | solution.py:208
  20.4 11.2 %collective-permute-start.3 = (f32[2,384,128]{2,1,0:T(8,128)S(1)}, f32[2,384,128]{2,1,0:T(8,128)S(1)}, u32[]{:S(2)}, u32[]{:S(2)}) collective-permute-start(f32[2,384,128]{2,1,0:T(8,128)S(1)} %get-tuple-element.29), channel_id=1, source_target_pairs={{1,2},{3,4},{5,6},{7,8},{9,10},{11,12},{13,14},{15,16},{17,18},{19... | collective-permute-start | bytes 1179656 | tf_op jit(solution)/shard_map/ppermute | solution.py:208
  43.3 8.7 %collective-permute-start.4 = (f32[2,64,384]{2,1,0:T(8,128)S(1)}, f32[2,64,384]{2,1,0:T(8,128)S(1)}, u32[]{:S(2)}, u32[]{:S(2)}) collective-permute-start(f32[2,64,384]{2,1,0:T(8,128)S(1)} %get-tuple-element.18), channel_id=1, source_target_pairs={{0,32},{64,96},{128,160},{192,224},{32,0},{96,64},{160,128},{224,1... | collective-permute-start | bytes 589832 | tf_op jit(solution)/shard_map/ppermute | solution.py:208
  43.4 14.0 %collective-permute-start.5 = (f32[2,64,384]{2,1,0:T(8,128)S(1)}, f32[2,64,384]{2,1,0:T(8,128)S(1)}, u32[]{:S(2)}, u32[]{:S(2)}) collective-permute-start(f32[2,64,384]{2,1,0:T(8,128)S(1)} %get-tuple-element.19), channel_id=1, source_target_pairs={{32,64},{96,128},{160,192},{64,32},{128,96},{192,160},{33,65},{97,... | collective-permute-start | bytes 589832 | tf_op jit(solution)/shard_map/ppermute | solution.py:208
  51.9 8.6 %collective-permute-start.10 = (f32[640,128]{1,0:T(8,128)S(1)}, f32[640,128]{1,0:T(8,128)}, u32[]{:S(2)}, u32[]{:S(2)}) collective-permute-start(f32[640,128]{1,0:T(8,128)S(1)} %get-tuple-element.11), channel_id=1, source_target_pairs={{0,1},{1,0},{2,3},{3,2},{4,5},{5,4},{6,7},{7,6},{8,9},{9,8},{10,11... | collective-permute-start | bytes 983048 | tf_op jit(solution)/shard_map/ppermute | solution.py:244
  58.6 11.9 %collective-permute-start.6 = (f32[2,256,128]{2,1,0:T(8,128)}, f32[2,256,128]{2,1,0:T(8,128)}, u32[]{:S(2)}, u32[]{:S(2)}) collective-permute-start(f32[2,256,128]{2,1,0:T(8,128)} %get-tuple-element.24), channel_id=1, source_target_pairs={{0,1},{2,3},{4,5},{6,7},{8,9},{10,11},{12,13},{14,15},{16,17},{18,... | collective-permute-start | bytes 786440 | tf_op jit(solution)/shard_map/ppermute | solution.py:208
  58.6 11.9 %collective-permute-start.7 = (f32[2,256,128]{2,1,0:T(8,128)}, f32[2,256,128]{2,1,0:T(8,128)}, u32[]{:S(2)}, u32[]{:S(2)}) collective-permute-start(f32[2,256,128]{2,1,0:T(8,128)} %get-tuple-element.25), channel_id=1, source_target_pairs={{1,2},{3,4},{5,6},{7,8},{9,10},{11,12},{13,14},{15,16},{17,18},{19... | collective-permute-start | bytes 786440 | tf_op jit(solution)/shard_map/ppermute | solution.py:208
  62.3 12.1 %all-to-all-start = ((f32[16,40,128]{2,1,0:T(8,128)}), f32[16,40,128]{2,1,0:T(8,128)S(1)}, u32[]{:S(2)}, u32[]{:S(2)}) async-start(f32[16,40,128]{2,1,0:T(8,128)} %bitcast.5), calls=%async_computation | async-start | bytes 655360 | tf_op jit(solution)/shard_map/all_to_all | solution.py:235
  75.1 18.8 %all-to-all-start.1 = ((f32[8,40,128]{2,1,0:T(8,128)}), f32[8,40,128]{2,1,0:T(8,128)S(1)}, u32[]{:S(2)}, u32[]{:S(2)}) async-start(f32[8,40,128]{2,1,0:T(8,128)} %broadcast_in_dim.22), calls=%async_computation.1 | async-start | bytes 327680 | tf_op jit(solution)/shard_map/all_to_all | solution.py:235
  85.3 24.6 %copy-start.13 = (f32[2,384,128]{2,1,0:T(8,128)S(1)}, f32[2,384,128]{2,1,0:T(8,128)}, u32[]{:S(2)}) copy-start(f32[2,384,128]{2,1,0:T(8,128)} %copy-done.12) | copy-start | bytes 1179652
  86.1 23.9 %copy-start.11 = (f32[2,256,384]{2,1,0:T(8,128)S(1)}, f32[2,256,384]{2,1,0:T(8,128)}, u32[]{:S(2)}) copy-start(f32[2,256,384]{2,1,0:T(8,128)} %copy-done.10) | copy-start | bytes 2359300
  86.1 16.1 %collective-permute-start.8 = (f32[2,64,384]{2,1,0:T(8,128)}, f32[2,64,384]{2,1,0:T(8,128)}, u32[]{:S(2)}, u32[]{:S(2)}) collective-permute-start(f32[2,64,384]{2,1,0:T(8,128)} %get-tuple-element.22), channel_id=1, source_target_pairs={{0,32},{64,96},{128,160},{192,224},{32,0},{96,64},{160,128},{224,1... | collective-permute-start | bytes 589832 | tf_op jit(solution)/shard_map/ppermute | solution.py:208
  86.8 17.5 %collective-permute-start.9 = (f32[2,64,384]{2,1,0:T(8,128)}, f32[2,64,384]{2,1,0:T(8,128)}, u32[]{:S(2)}, u32[]{:S(2)}) collective-permute-start(f32[2,64,384]{2,1,0:T(8,128)} %get-tuple-element.23), channel_id=1, source_target_pairs={{32,64},{96,128},{160,192},{64,32},{128,96},{192,160},{33,65},{97,... | collective-permute-start | bytes 589832 | tf_op jit(solution)/shard_map/ppermute | solution.py:208
  94.7 11.4 %all-to-all-start.2 = ((f32[16,40,128]{2,1,0:T(8,128)}), f32[16,40,128]{2,1,0:T(8,128)S(1)}, u32[]{:S(2)}, u32[]{:S(2)}) async-start(f32[16,40,128]{2,1,0:T(8,128)} %broadcast_in_dim.23), calls=%async_computation.2 | async-start | bytes 655360 | tf_op jit(solution)/shard_map/all_to_all | solution.py:235
  106.1 6.8 %collective-permute-start.11 = (f32[640,128]{1,0:T(8,128)S(1)}, f32[640,128]{1,0:T(8,128)S(1)}, u32[]{:S(2)}, u32[]{:S(2)}) collective-permute-start(f32[640,128]{1,0:T(8,128)S(1)} %bitcast.16), channel_id=1, source_target_pairs={{0,1},{1,0},{2,3},{3,2},{4,5},{5,4},{6,7},{7,6},{8,9},{9,8},{10,11... | collective-permute-start | bytes 983048 | tf_op jit(solution)/shard_map/ppermute | solution.py:244
  123.8 1.7 collective-permute-start.16
  126.2 13.5 %all-to-all-start.3 = ((f32[16,40,128]{2,1,0:T(8,128)}), f32[16,40,128]{2,1,0:T(8,128)S(1)}, u32[]{:S(2)}, u32[]{:S(2)}) async-start(f32[16,40,128]{2,1,0:T(8,128)} %bitcast.7), calls=%async_computation.3 | async-start | bytes 655360 | tf_op jit(solution)/shard_map/all_to_all | solution.py:235
  132.5 11.9 %collective-permute-start.12 = (f32[2,64,384]{2,1,0:T(8,128)S(1)}, f32[2,64,384]{2,1,0:T(8,128)S(1)}, u32[]{:S(2)}, u32[]{:S(2)}) collective-permute-start(f32[2,64,384]{2,1,0:T(8,128)S(1)} %get-tuple-element.16), channel_id=1, source_target_pairs={{0,32},{64,96},{128,160},{192,224},{32,0},{96,64},{160,128},{224,1... | collective-permute-start | bytes 589832 | tf_op jit(solution)/shard_map/ppermute | solution.py:208
  133.2 19.0 %collective-permute-start.13 = (f32[2,64,384]{2,1,0:T(8,128)S(1)}, f32[2,64,384]{2,1,0:T(8,128)S(1)}, u32[]{:S(2)}, u32[]{:S(2)}) collective-permute-start(f32[2,64,384]{2,1,0:T(8,128)S(1)} %get-tuple-element.17), channel_id=1, source_target_pairs={{32,64},{96,128},{160,192},{64,32},{128,96},{192,160},{33,65},{97,... | collective-permute-start | bytes 589832 | tf_op jit(solution)/shard_map/ppermute | solution.py:208
  140.5 12.0 %all-to-all-start.4 = ((f32[8,40,128]{2,1,0:T(8,128)}), f32[8,40,128]{2,1,0:T(8,128)S(1)}, u32[]{:S(2)}, u32[]{:S(2)}) async-start(f32[8,40,128]{2,1,0:T(8,128)} %broadcast_in_dim.40), calls=%async_computation.4 | async-start | bytes 327680 | tf_op jit(solution)/shard_map/all_to_all | solution.py:235
  153.3 12.3 %all-to-all-start.5 = ((f32[16,40,128]{2,1,0:T(8,128)}), f32[16,40,128]{2,1,0:T(8,128)S(1)}, u32[]{:S(2)}, u32[]{:S(2)}) async-start(f32[16,40,128]{2,1,0:T(8,128)} %broadcast_in_dim.41), calls=%async_computation.5 | async-start | bytes 655360 | tf_op jit(solution)/shard_map/all_to_all | solution.py:235
  159.8 7.8 %collective-permute-start.14 = (f32[2,256,64]{2,1,0:T(8,128)S(1)}, f32[2,256,64]{2,1,0:T(8,128)S(1)}, u32[]{:S(2)}, u32[]{:S(2)}) collective-permute-start(f32[2,256,64]{2,1,0:T(8,128)S(1)} %get-tuple-element.20), channel_id=1, source_target_pairs={{0,1},{2,3},{4,5},{6,7},{8,9},{10,11},{12,13},{14,15},{16,17},{18,... | collective-permute-start | bytes 393224 | tf_op jit(solution)/shard_map/ppermute | solution.py:208
  162.9 9.8 %collective-permute-start.15 = (f32[2,256,64]{2,1,0:T(8,128)S(1)}, f32[2,256,64]{2,1,0:T(8,128)S(1)}, u32[]{:S(2)}, u32[]{:S(2)}) collective-permute-start(f32[2,256,64]{2,1,0:T(8,128)S(1)} %get-tuple-element.21), channel_id=1, source_target_pairs={{1,2},{3,4},{5,6},{7,8},{9,10},{11,12},{13,14},{15,16},{17,18},{19... | collective-permute-start | bytes 393224 | tf_op jit(solution)/shard_map/ppermute | solution.py:208
  165.6 9.3 %collective-permute-start.17 = (f32[640,128]{1,0:T(8,128)S(1)}, f32[640,128]{1,0:T(8,128)S(1)}, u32[]{:S(2)}, u32[]{:S(2)}) collective-permute-start(f32[640,128]{1,0:T(8,128)S(1)} %bitcast.19), channel_id=1, source_target_pairs={{0,1},{1,0},{2,3},{3,2},{4,5},{5,4},{6,7},{7,6},{8,9},{9,8},{10,11... | collective-permute-start | bytes 983048 | tf_op jit(solution)/shard_map/ppermute | solution.py:244
  (11 other events, 19.7 us)

commit v2 on v0

--- a/solution.py
+++ b/solution.py
@@ -199,16 +199,22 @@
     )(starts, count, core, *operands)
 
 
-def neighbours(low_strip, high_strip, axis):
+def neighbours(low_strip, high_strip, axis, apart=False):
     count = lax.axis_size(axis)
     odd = lax.axis_index(axis) % 2 == 1
 
-    def meet(block, start):
-        pairs = [(i, i + 1) for i in range(start, count - 1, 2)]
+    def meet(block, pairs):
         return lax.ppermute(block, axis, pairs + [(j, i) for i, j in pairs])
 
-    first = meet(jnp.where(odd, high_strip, low_strip), 1)
-    second = meet(jnp.where(odd, low_strip, high_strip), 0)
+    middle = [(count // 2 - 1, count // 2)]
+    pairs = [(i, i + 1) for i in range(1, count - 1, 2)]
+    block = jnp.where(odd, high_strip, low_strip)
+    first = meet(block, middle if apart else pairs)
+    if apart:
+        first = first + meet(block, [pair for pair in pairs if pair not in middle])
+    second = meet(
+        jnp.where(odd, low_strip, high_strip), [(i, i + 1) for i in range(0, count - 1, 2)]
+    )
     return jnp.where(odd, second, first), jnp.where(odd, first, second)
 
 
@@ -278,20 +284,20 @@
     low, high = neighbours(at(frame, 2, 0, LANES), at(frame, 2, cols - LANES, cols), "col")
     frame = jnp.concatenate([low, frame, high], axis=2)
 
-    at_row = lax.broadcasted_iota(jnp.int32, (1, tall, 1), 1) + (lax.axis_index("row") * rows - rim)
-    at_col = lax.broadcasted_iota(jnp.int32, (1, 1, wide), 2) + (lax.axis_index("col") * cols - LANES)
-    inside = (at_row >= 0) & (at_row < rows * lax.axis_size("row"))
-    inside = inside & (at_col >= 0) & (at_col < cols * lax.axis_size("col"))
     core = (lax.axis_index("col") % CORES).reshape(1)
     left, right = margin, LANES + cols + rim
     updates, mine, other = run_pass(starts, count, core, frame, probe, None, amplitude, tables, margin)
     means = total(mine, other)
     strips = at(updates, 2, left, right)
+    low, high = neighbours(at(strips, 1, 0, 2 * rim), at(strips, 1, rows, tall), "row", True)
+    strips = strips + padded(low, 1, 0, tall) + padded(high, 1, rows, tall)
     low, high = neighbours(at(strips, 2, 0, 2 * rim), at(strips, 2, cols, cols + 2 * rim), "col")
     strips = strips + padded(low, 2, 0, cols + 2 * rim) + padded(high, 2, cols, cols + 2 * rim)
-    low, high = neighbours(at(strips, 1, 0, 2 * rim), at(strips, 1, rows, tall), "row")
-    strips = strips + padded(low, 1, 0, tall) + padded(high, 1, rows, tall)
     updates = padded(strips, 2, left, wide)
+    at_row = lax.broadcasted_iota(jnp.int32, (1, tall, 1), 1) + (lax.axis_index("row") * rows - rim)
+    at_col = lax.broadcasted_iota(jnp.int32, (1, 1, wide), 2) + (lax.axis_index("col") * cols - LANES)
+    inside = (at_row >= 0) & (at_row < rows * lax.axis_size("row"))
+    inside = inside & (at_col >= 0) & (at_col < cols * lax.axis_size("col"))
     frame = frame + jnp.where(inside, updates, 0.0)
 
     updates, mine, other, probe = run_pass(
@@ -299,12 +305,12 @@
     )
     mine, other = total(mine, other)
     strips = at(updates, 2, left, right)
-    low, high = neighbours(at(strips, 2, 0, rim), at(strips, 2, rim + cols, cols + 2 * rim), "col")
-    middle = at(strips, 2, rim, rim + cols)
-    middle = middle + padded(low, 2, 0, cols) + padded(high, 2, cols - rim, cols)
-    low, high = neighbours(at(middle, 1, 0, rim), at(middle, 1, tall - rim, tall), "row")
-    tile = at(middle, 1, rim, rim + rows)
-    tile = tile + padded(low, 1, 0, rows) + padded(high, 1, rows - rim, rows)
+    low, high = neighbours(at(strips, 1, 0, rim), at(strips, 1, tall - rim, tall), "row", True)
+    middle = at(strips, 1, rim, rim + rows)
+    middle = middle + padded(low, 1, 0, rows) + padded(high, 1, rows - rim, rows)
+    low, high = neighbours(at(middle, 2, 0, rim), at(middle, 2, rim + cols, cols + 2 * rim), "col")
+    tile = at(middle, 2, rim, rim + cols)
+    tile = tile + padded(low, 2, 0, cols) + padded(high, 2, cols - rim, cols)
     object_out = frame[:, rim : rim + rows, LANES : LANES + cols] + tile
     lower = jnp.where(core[0] == 0, mine, other)
     upper = jnp.where(core[0] == 0, other, mine)

time: 177 us -> 173 us (0.977)
  the two profiles are of different devices: /device:TPU:6 before, /device:TPU:25 now
where the time goes in v2:
time: 173 us; the launch traced here: 172 us
  starting transfers between devices  94.9 us (55%)
  waiting for transfers between devices  36.8 us (21%)
  other arithmetic  21.5 us (12%)
  Pallas kernels  12.2 us (7%)
  local copies, waits for them, and re-layouts  4.41 us (3%)
  between operations  1.79 us (1%)
    all_to_all x6, starting transfers between devices, exchange(): lax.all_to_all(blocks, AXES, 0, 0, axis_index_groups=members, tiled=True)  55.9 us
    ppermute x14, starting transfers between devices, meet(): return lax.ppermute(block, axis, pairs + [(j, i) for i, j in pairs])  30.8 us
    all_to_all x6, waiting for transfers between devices, exchange(): lax.all_to_all(blocks, AXES, 0, 0, axis_index_groups=members, tiled=True)  20.1 us
    ppermute x14, waiting for transfers between devices, meet(): return lax.ppermute(block, axis, pairs + [(j, i) for i, j in pairs])  13.3 us
    pallas_call x2, Pallas kernels, run_pass(): pl.pallas_call(functools.partial(pass_kernel, modes=modes, size=size, mar...  12.2 us
    ppermute x4, starting transfers between devices, swap(): return lax.ppermute(block, 'col', [(i, i ^ 1) for i in range(count)])  8.25 us
  transfers between devices with their start and end apart: 24, of which 12 were waited for; matrix products, arithmetic and copies ran while one was open for 10% of the time, Pallas kernels for 0%

profile of v2, /device:TPU:25, one launch (start us, length us, event | category | flops | bytes accessed | tf_op | source)
XLA Modules:
  0.0 171.6 jit_solution(5840258578153136175)
XLA Ops:
  3.6 2.5 %collective-permute-done = f32[2,64,256]{2,1,0:T(8,128)S(1)} collective-permute-done((f32[2,64,256]{2,1,0:T(8,128)S(1)}, f32[2,64,256]{2,1,0:T(8,128)S(1)}, u32[]{:S(2)}, u32[]{:S(2)}) %collective-permute-start) | collective-permute-done | bytes 131104 | tf_op jit(solution)/shard_map/ppermute | solution.py:207
  7.5 1.6 collective-permute-start.2
  9.1 3.2 %collective-permute-start.3 = (f32[2,384,128]{2,1,0:T(8,128)S(1)}, f32[2,384,128]{2,1,0:T(8,128)S(1)}, u32[]{:S(2)}, u32[]{:S(2)}) collective-permute-start(f32[2,384,128]{2,1,0:T(8,128)S(1)} %get-tuple-element.31), channel_id=1, source_target_pairs={{1,2},{3,4},{5,6},{7,8},{9,10},{11,12},{13,14},{15,16},{17,18},{19... | collective-permute-start | bytes 1179656 | tf_op jit(solution)/shard_map/ppermute | solution.py:207
  13.3 7.0 %collective-permute-done.3 = f32[2,384,128]{2,1,0:T(8,128)S(1)} collective-permute-done((f32[2,384,128]{2,1,0:T(8,128)S(1)}, f32[2,384,128]{2,1,0:T(8,128)S(1)}, u32[]{:S(2)}, u32[]{:S(2)}) %collective-permute-start.3) | collective-permute-done | bytes 393248 | tf_op jit(solution)/shard_map/ppermute | solution.py:207
  21.8 5.6 %shard_map.113 = (f32[2,384,512]{2,1,0:T(8,128)S(1)}, f32[640,128]{1,0:T(8,128)S(1)}, f32[640,128]{1,0:T(8,128)S(1)}) custom-call(s32[8,2]{1,0:T(8,128)S(1)} %copy.14.refs_0_, s32[1]{0:T(128)} %bitcast.14.refs_1_, s32[1]{0:T(128)} %bitcast.2.refs_2_, f32[2,384,512]{2,1,0:T(8,128)S(1)} %pad_maximum_fusion.refs_3_, f32[2,4,128,128]{3,2,1,0:T(8,128)S(1)} %copy-done, ...), custom_call_target="tpu_custom_call" | custom-call | flops 6442450944 | bytes 6291456 | tf_op jit(solution)/shard_map/pallas_call | solution.py:191
  28.6 8.3 %collective-permute-start.4 = (f32[2,128,384]{2,1,0:T(8,128)}, f32[2,128,384]{2,1,0:T(8,128)}, u32[]{:S(2)}, u32[]{:S(2)}) collective-permute-start(f32[2,128,384]{2,1,0:T(8,128)} %get-tuple-element.19), channel_id=1, source_target_pairs={{0,32},{64,96},{128,160},{192,224},{32,0},{96,64},{160,128},{224,1... | collective-permute-start | bytes 1179656 | tf_op jit(solution)/shard_map/ppermute | solution.py:207
  39.8 1.8 %collective-permute-done.9 = f32[640,128]{1,0:T(8,128)} collective-permute-done((f32[640,128]{1,0:T(8,128)S(1)}, f32[640,128]{1,0:T(8,128)}, u32[]{:S(2)}, u32[]{:S(2)}) %collective-permute-start.9) | collective-permute-done | bytes 327712 | tf_op jit(solution)/shard_map/ppermute | solution.py:250
  41.6 1.7 %add.114 = f32[640,128]{1,0:T(8,128)} add(f32[640,128]{1,0:T(8,128)S(1)} %get-tuple-element.10, f32[640,128]{1,0:T(8,128)} %collective-permute-done.9) | non-fusion elementwise | flops 81920 | bytes 983040 | tf_op jit(solution)/shard_map/add | solution.py:255
  43.3 18.9 %all-to-all-start = ((f32[16,40,128]{2,1,0:T(8,128)}), f32[16,40,128]{2,1,0:T(8,128)S(1)}, u32[]{:S(2)}, u32[]{:S(2)}) async-start(f32[16,40,128]{2,1,0:T(8,128)} %bitcast.5), calls=%async_computation | async-start | bytes 655360 | tf_op jit(solution)/shard_map/all_to_all | solution.py:241
  63.6 1.5 pad_add_fusion.1
  65.0 3.8 %all-to-all-done = f32[16,40,128]{2,1,0:T(8,128)S(1)} async-done(((f32[16,40,128]{2,1,0:T(8,128)}), f32[16,40,128]{2,1,0:T(8,128)S(1)}, u32[]{:S(2)}, u32[]{:S(2)}) %all-to-all-start) | async-done | bytes 327712 | tf_op jit(solution)/shard_map/all_to_all | solution.py:241
  69.6 12.3 %all-to-all-start.1 = ((f32[8,40,128]{2,1,0:T(8,128)}), f32[8,40,128]{2,1,0:T(8,128)S(1)}, u32[]{:S(2)}, u32[]{:S(2)}) async-start(f32[8,40,128]{2,1,0:T(8,128)} %broadcast_in_dim.22), calls=%async_computation.1 | async-start | bytes 327680 | tf_op jit(solution)/shard_map/all_to_all | solution.py:241
  81.9 2.0 %slice_select_fusion.1 = (f32[2,384,128]{2,1,0:T(8,128)}, f32[2,384,128]{2,1,0:T(8,128)}) fusion(f32[2,384,384]{2,1,0:T(8,128)} %pad_add_fusion.1, pred[]{:T(512)S(6)} %eq.22), kind=kLoop, calls=%fused_computation.14 | loop fusion | flops 196608 | bytes 1572865 | tf_op jit(solution)/shard_map/jit(_where)/select_n | solution.py:216
  84.8 3.9 %collective-permute-start.8 = (f32[2,384,128]{2,1,0:T(8,128)}, f32[2,384,128]{2,1,0:T(8,128)}, u32[]{:S(2)}, u32[]{:S(2)}) collective-permute-start(f32[2,384,128]{2,1,0:T(8,128)} %get-tuple-element.21), channel_id=1, source_target_pairs={{1,2},{3,4},{5,6},{7,8},{9,10},{11,12},{13,14},{15,16},{17,18},{19... | collective-permute-start | bytes 1179656 | tf_op jit(solution)/shard_map/ppermute | solution.py:207
  88.7 1.6 all-to-all-done.1
  91.1 4.0 %all-to-all-start.2 = ((f32[16,40,128]{2,1,0:T(8,128)}), f32[16,40,128]{2,1,0:T(8,128)S(1)}, u32[]{:S(2)}, u32[]{:S(2)}) async-start(f32[16,40,128]{2,1,0:T(8,128)} %broadcast_in_dim.23), calls=%async_computation.2 | async-start | bytes 655360 | tf_op jit(solution)/shard_map/all_to_all | solution.py:241
  96.4 1.9 %broadcast_select_fusion.3 = (f32[2,384,128]{2,1,0:T(8,128)}, f32[2,384,128]{2,1,0:T(8,128)}) fusion(f32[2,384,128]{2,1,0:T(8,128)S(1)} %collective-permute-done.7, f32[2,384,128]{2,1,0:T(8,128)} %collective-permute-done.8, pred[]{:T(512)S(6)} %eq.22), kind=kLoop, calls=%fused_computation.24 | loop fusion | flops 196608 | bytes 1572865 | tf_op jit(solution)/shard_map/jit(_where)/select_n | solution.py:218
  98.3 2.6 %all-to-all-done.2 = f32[16,40,128]{2,1,0:T(8,128)S(1)} async-done(((f32[16,40,128]{2,1,0:T(8,128)}), f32[16,40,128]{2,1,0:T(8,128)S(1)}, u32[]{:S(2)}, u32[]{:S(2)}) %all-to-all-start.2) | async-done | bytes 327712 | tf_op jit(solution)/shard_map/all_to_all | solution.py:241
  100.8 3.8 %collective-permute-start.10 = (f32[640,128]{1,0:T(8,128)S(1)}, f32[640,128]{1,0:T(8,128)S(1)}, u32[]{:S(2)}, u32[]{:S(2)}) collective-permute-start(f32[640,128]{1,0:T(8,128)S(1)} %bitcast.16), channel_id=1, source_target_pairs={{0,1},{1,0},{2,3},{3,2},{4,5},{5,4},{6,7},{7,6},{8,9},{9,8},{10,11... | collective-permute-start | bytes 983048 | tf_op jit(solution)/shard_map/ppermute | solution.py:250
  106.3 1.7 select_add_fusion.refs_3_
  108.0 6.5 %shard_map.114 = (f32[2,384,512]{2,1,0:T(8,128)S(1)}, f32[640,128]{1,0:T(8,128)S(1)}, f32[640,128]{1,0:T(8,128)S(1)}, f32[2,4,128,128]{3,2,1,0:T(8,128)S(1)}) custom-call(s32[8,2]{1,0:T(8,128)S(1)} %copy.14.refs_0_, s32[1]{0:T(128)} %bitcast.15.refs_1_, s32[1]{0:T(128)} %bitcast.2.refs_2_, f32[2,384,512]{2,1,0:T(8,128)} %select_add_fusion.refs_3_, ...), custom_call_target="tpu_custom_call" | custom-call | flops 6442450944 | bytes 6291456 | tf_op jit(solution)/shard_map/pallas_call | solution.py:191
  114.6 1.6 collective-permute-done.16
  117.0 9.9 %all-to-all-start.3 = ((f32[16,40,128]{2,1,0:T(8,128)}), f32[16,40,128]{2,1,0:T(8,128)S(1)}, u32[]{:S(2)}, u32[]{:S(2)}) async-start(f32[16,40,128]{2,1,0:T(8,128)} %bitcast.7), calls=%async_computation.3 | async-start | bytes 655360 | tf_op jit(solution)/shard_map/all_to_all | solution.py:241
  130.3 3.3 %all-to-all-done.3 = f32[16,40,128]{2,1,0:T(8,128)S(1)} async-done(((f32[16,40,128]{2,1,0:T(8,128)}), f32[16,40,128]{2,1,0:T(8,128)S(1)}, u32[]{:S(2)}, u32[]{:S(2)}) %all-to-all-start.3) | async-done | bytes 327712 | tf_op jit(solution)/shard_map/all_to_all | solution.py:241
  134.3 6.1 %all-to-all-start.4 = ((f32[8,40,128]{2,1,0:T(8,128)}), f32[8,40,128]{2,1,0:T(8,128)S(1)}, u32[]{:S(2)}, u32[]{:S(2)}) async-start(f32[8,40,128]{2,1,0:T(8,128)} %broadcast_in_dim.40), calls=%async_computation.4 | async-start | bytes 327680 | tf_op jit(solution)/shard_map/all_to_all | solution.py:241
  140.8 8.6 %all-to-all-done.4 = f32[8,40,128]{2,1,0:T(8,128)S(1)} async-done(((f32[8,40,128]{2,1,0:T(8,128)}), f32[8,40,128]{2,1,0:T(8,128)S(1)}, u32[]{:S(2)}, u32[]{:S(2)}) %all-to-all-start.4) | async-done | bytes 163872 | tf_op jit(solution)/shard_map/all_to_all | solution.py:241
  150.1 4.7 %all-to-all-start.5 = ((f32[16,40,128]{2,1,0:T(8,128)}), f32[16,40,128]{2,1,0:T(8,128)S(1)}, u32[]{:S(2)}, u32[]{:S(2)}) async-start(f32[16,40,128]{2,1,0:T(8,128)} %broadcast_in_dim.41), calls=%async_computation.5 | async-start | bytes 655360 | tf_op jit(solution)/shard_map/all_to_all | solution.py:241
  155.0 3.6 %collective-permute-start.14 = (f32[2,256,64]{2,1,0:T(8,128)S(1)}, f32[2,256,64]{2,1,0:T(8,128)S(1)}, u32[]{:S(2)}, u32[]{:S(2)}) collective-permute-start(f32[2,256,64]{2,1,0:T(8,128)S(1)} %get-tuple-element.24), channel_id=1, source_target_pairs={{0,1},{2,3},{4,5},{6,7},{8,9},{10,11},{12,13},{14,15},{16,17},{18,... | collective-permute-start | bytes 393224 | tf_op jit(solution)/shard_map/ppermute | solution.py:207
  158.6 1.9 %collective-permute-start.15 = (f32[2,256,64]{2,1,0:T(8,128)S(1)}, f32[2,256,64]{2,1,0:T(8,128)S(1)}, u32[]{:S(2)}, u32[]{:S(2)}) collective-permute-start(f32[2,256,64]{2,1,0:T(8,128)S(1)} %get-tuple-element.25), channel_id=1, source_target_pairs={{1,2},{3,4},{5,6},{7,8},{9,10},{11,12},{13,14},{15,16},{17,18},{19... | collective-permute-start | bytes 393224 | tf_op jit(solution)/shard_map/ppermute | solution.py:207
  160.7 4.4 %collective-permute-start.17 = (f32[640,128]{1,0:T(8,128)S(1)}, f32[640,128]{1,0:T(8,128)S(1)}, u32[]{:S(2)}, u32[]{:S(2)}) collective-permute-start(f32[640,128]{1,0:T(8,128)S(1)} %bitcast.19), channel_id=1, source_target_pairs={{0,1},{1,0},{2,3},{3,2},{4,5},{5,4},{6,7},{7,6},{8,9},{9,8},{10,11... | collective-permute-start | bytes 983048 | tf_op jit(solution)/shard_map/ppermute | solution.py:250
  165.1 3.3 %collective-permute-done.15 = f32[2,256,64]{2,1,0:T(8,128)S(1)} collective-permute-done((f32[2,256,64]{2,1,0:T(8,128)S(1)}, f32[2,256,64]{2,1,0:T(8,128)S(1)}, u32[]{:S(2)}, u32[]{:S(2)}) %collective-permute-start.15) | collective-permute-done | bytes 131104 | tf_op jit(solution)/shard_map/ppermute | solution.py:207
  168.5 2.1 %fusion.1 = f32[2,256,256]{2,1,0:T(8,128)} fusion(f32[2,256,384]{2,1,0:T(8,128)S(1)} %pad_add_fusion.2, f32[2,384,512]{2,1,0:T(8,128)} %select_add_fusion.refs_3_, f32[2,256,64]{2,1,0:T(8,128)S(1)} %get-tuple-element.37, f32[2,256,64]{2,1,0:T(8,128)S(1)} %get-tuple-element.36), kind=kLoop, calls=%fused_computation.10 | loop fusion | flops 393216 | bytes 1835008 | tf_op jit(solution)/shard_map/add | solution.py:314
  (104 shorter events, 23.9 us)
Async XLA Ops:
  1.6 4.5 %collective-permute-start = (f32[2,64,256]{2,1,0:T(8,128)S(1)}, f32[2,64,256]{2,1,0:T(8,128)S(1)}, u32[]{:S(2)}, u32[]{:S(2)}) collective-permute-start(f32[2,64,256]{2,1,0:T(8,128)S(1)} %get-tuple-element.38), channel_id=1, source_target_pairs={{0,32},{64,96},{128,160},{192,224},{32,0},{96,64},{160,128},{224,1... | collective-permute-start | bytes 393224 | tf_op jit(solution)/shard_map/ppermute | solution.py:207
  2.9 3.2 %collective-permute-start.1 = (f32[2,64,256]{2,1,0:T(8,128)S(1)}, f32[2,64,256]{2,1,0:T(8,128)S(1)}, u32[]{:S(2)}, u32[]{:S(2)}) collective-permute-start(f32[2,64,256]{2,1,0:T(8,128)S(1)} %get-tuple-element.39), channel_id=1, source_target_pairs={{32,64},{96,128},{160,192},{64,32},{128,96},{192,160},{33,65},{97,... | collective-permute-start | bytes 393224 | tf_op jit(solution)/shard_map/ppermute | solution.py:207
  6.1 14.2 %copy-start.16 = (f32[2,64,256]{2,1,0:T(8,128)}, f32[2,64,256]{2,1,0:T(8,128)S(1)}, u32[]{:S(2)}) copy-start(f32[2,64,256]{2,1,0:T(8,128)S(1)} %get-tuple-element.40) | copy-start | bytes 393220
  6.2 14.2 %copy-start.18 = (f32[2,64,256]{2,1,0:T(8,128)}, f32[2,64,256]{2,1,0:T(8,128)S(1)}, u32[]{:S(2)}) copy-start(f32[2,64,256]{2,1,0:T(8,128)S(1)} %get-tuple-element.41) | copy-start | bytes 393220
  6.2 6.2 %copy-start.23 = (s32[1,1,8,2]{2,3,1,0:T(2,128)S(1)}, s32[1,1,8,2]{2,3,1,0:T(2,128)}, u32[]{:S(2)}) copy-start(s32[1,1,8,2]{2,3,1,0:T(2,128)} %param.14) | copy-start | bytes 196
  6.2 6.9 %copy-start.21 = (bf16[1,1,8,128,128]{4,3,2,1,0:T(8,128)(2,1)S(1)}, bf16[1,1,8,128,128]{4,3,2,1,0:T(8,128)(2,1)}, u32[]{:S(2)}) copy-start(bf16[1,1,8,128,128]{4,3,2,1,0:T(8,128)(2,1)} %param.12) | copy-start | bytes 786436
  6.2 6.9 %copy-start.22 = (f32[1,1,8,128]{3,2,1,0:T(8,128)S(1)}, f32[1,1,8,128]{3,2,1,0:T(8,128)}, u32[]{:S(2)}) copy-start(f32[1,1,8,128]{3,2,1,0:T(8,128)} %param.13) | copy-start | bytes 12292
  7.5 12.9 %copy-start.10 = (f32[2,256,256]{2,1,0:T(8,128)S(1)}, f32[2,256,256]{2,1,0:T(8,128)}, u32[]{:S(2)}) copy-start(f32[2,256,256]{2,1,0:T(8,128)} %param.10) | copy-start | bytes 1572868
  7.5 5.8 %collective-permute-start.2 = (f32[2,384,128]{2,1,0:T(8,128)S(1)}, f32[2,384,128]{2,1,0:T(8,128)S(1)}, u32[]{:S(2)}, u32[]{:S(2)}) collective-permute-start(f32[2,384,128]{2,1,0:T(8,128)S(1)} %get-tuple-element.30), channel_id=1, source_target_pairs={{0,1},{2,3},{4,5},{6,7},{8,9},{10,11},{12,13},{14,15},{16,17},{18,... | collective-permute-start | bytes 1179656 | tf_op jit(solution)/shard_map/ppermute | solution.py:207
  9.1 11.2 %collective-permute-start.3 = (f32[2,384,128]{2,1,0:T(8,128)S(1)}, f32[2,384,128]{2,1,0:T(8,128)S(1)}, u32[]{:S(2)}, u32[]{:S(2)}) collective-permute-start(f32[2,384,128]{2,1,0:T(8,128)S(1)} %get-tuple-element.31), channel_id=1, source_target_pairs={{1,2},{3,4},{5,6},{7,8},{9,10},{11,12},{13,14},{15,16},{17,18},{19... | collective-permute-start | bytes 1179656 | tf_op jit(solution)/shard_map/ppermute | solution.py:207
  28.6 33.6 %collective-permute-start.4 = (f32[2,128,384]{2,1,0:T(8,128)}, f32[2,128,384]{2,1,0:T(8,128)}, u32[]{:S(2)}, u32[]{:S(2)}) collective-permute-start(f32[2,128,384]{2,1,0:T(8,128)} %get-tuple-element.19), channel_id=1, source_target_pairs={{0,32},{64,96},{128,160},{192,224},{32,0},{96,64},{160,128},{224,1... | collective-permute-start | bytes 1179656 | tf_op jit(solution)/shard_map/ppermute | solution.py:207
  37.0 25.3 %collective-permute-start.5 = (f32[2,128,384]{2,1,0:T(8,128)}, f32[2,128,384]{2,1,0:T(8,128)}, u32[]{:S(2)}, u32[]{:S(2)}) collective-permute-start(f32[2,128,384]{2,1,0:T(8,128)} %get-tuple-element.18), channel_id=1, source_target_pairs={{96,128},{128,96},{97,129},{129,97},{98,130},{130,98},{99,131},{13... | collective-permute-start | bytes 1179656 | tf_op jit(solution)/shard_map/ppermute | solution.py:207
  38.4 23.8 %collective-permute-start.6 = (f32[2,128,384]{2,1,0:T(8,128)}, f32[2,128,384]{2,1,0:T(8,128)}, u32[]{:S(2)}, u32[]{:S(2)}) collective-permute-start(f32[2,128,384]{2,1,0:T(8,128)} %get-tuple-element.18), channel_id=1, source_target_pairs={{32,64},{160,192},{64,32},{192,160},{33,65},{161,193},{65,33},{193... | collective-permute-start | bytes 1179656 | tf_op jit(solution)/shard_map/ppermute | solution.py:207
  39.8 1.8 %collective-permute-start.9 = (f32[640,128]{1,0:T(8,128)S(1)}, f32[640,128]{1,0:T(8,128)}, u32[]{:S(2)}, u32[]{:S(2)}) collective-permute-start(f32[640,128]{1,0:T(8,128)S(1)} %get-tuple-element.11), channel_id=1, source_target_pairs={{0,1},{1,0},{2,3},{3,2},{4,5},{5,4},{6,7},{7,6},{8,9},{9,8},{10,11... | collective-permute-start | bytes 983048 | tf_op jit(solution)/shard_map/ppermute | solution.py:250
  43.3 25.5 %all-to-all-start = ((f32[16,40,128]{2,1,0:T(8,128)}), f32[16,40,128]{2,1,0:T(8,128)S(1)}, u32[]{:S(2)}, u32[]{:S(2)}) async-start(f32[16,40,128]{2,1,0:T(8,128)} %bitcast.5), calls=%async_computation | async-start | bytes 655360 | tf_op jit(solution)/shard_map/all_to_all | solution.py:241
  69.6 20.7 %all-to-all-start.1 = ((f32[8,40,128]{2,1,0:T(8,128)}), f32[8,40,128]{2,1,0:T(8,128)S(1)}, u32[]{:S(2)}, u32[]{:S(2)}) async-start(f32[8,40,128]{2,1,0:T(8,128)} %broadcast_in_dim.22), calls=%async_computation.1 | async-start | bytes 327680 | tf_op jit(solution)/shard_map/all_to_all | solution.py:241
  84.0 20.6 %copy-start.9 = (f32[2,384,384]{2,1,0:T(8,128)S(1)}, f32[2,384,384]{2,1,0:T(8,128)}, u32[]{:S(2)}) copy-start(f32[2,384,384]{2,1,0:T(8,128)} %pad_add_fusion.1) | copy-start | bytes 3538948
  84.0 11.9 %collective-permute-start.7 = (f32[2,384,128]{2,1,0:T(8,128)}, f32[2,384,128]{2,1,0:T(8,128)S(1)}, u32[]{:S(2)}, u32[]{:S(2)}) collective-permute-start(f32[2,384,128]{2,1,0:T(8,128)} %get-tuple-element.20), channel_id=1, source_target_pairs={{0,1},{2,3},{4,5},{6,7},{8,9},{10,11},{12,13},{14,15},{16,17},{18,... | collective-permute-start | bytes 1179656 | tf_op jit(solution)/shard_map/ppermute | solution.py:207
  84.8 11.5 %collective-permute-start.8 = (f32[2,384,128]{2,1,0:T(8,128)}, f32[2,384,128]{2,1,0:T(8,128)}, u32[]{:S(2)}, u32[]{:S(2)}) collective-permute-start(f32[2,384,128]{2,1,0:T(8,128)} %get-tuple-element.21), channel_id=1, source_target_pairs={{1,2},{3,4},{5,6},{7,8},{9,10},{11,12},{13,14},{15,16},{17,18},{19... | collective-permute-start | bytes 1179656 | tf_op jit(solution)/shard_map/ppermute | solution.py:207
  91.1 9.8 %all-to-all-start.2 = ((f32[16,40,128]{2,1,0:T(8,128)}), f32[16,40,128]{2,1,0:T(8,128)S(1)}, u32[]{:S(2)}, u32[]{:S(2)}) async-start(f32[16,40,128]{2,1,0:T(8,128)} %broadcast_in_dim.23), calls=%async_computation.2 | async-start | bytes 655360 | tf_op jit(solution)/shard_map/all_to_all | solution.py:241
  100.8 7.1 %collective-permute-start.10 = (f32[640,128]{1,0:T(8,128)S(1)}, f32[640,128]{1,0:T(8,128)S(1)}, u32[]{:S(2)}, u32[]{:S(2)}) collective-permute-start(f32[640,128]{1,0:T(8,128)S(1)} %bitcast.16), channel_id=1, source_target_pairs={{0,1},{1,0},{2,3},{3,2},{4,5},{5,4},{6,7},{7,6},{8,9},{9,8},{10,11... | collective-permute-start | bytes 983048 | tf_op jit(solution)/shard_map/ppermute | solution.py:250
  106.3 1.7 copy-start.8
  114.5 1.7 %collective-permute-start.16 = (f32[640,128]{1,0:T(8,128)S(1)}, f32[640,128]{1,0:T(8,128)S(1)}, u32[]{:S(2)}, u32[]{:S(2)}) collective-permute-start(f32[640,128]{1,0:T(8,128)S(1)} %get-tuple-element.15), channel_id=1, source_target_pairs={{0,1},{1,0},{2,3},{3,2},{4,5},{5,4},{6,7},{7,6},{8,9},{9,8},{10,11... | collective-permute-start | bytes 983048 | tf_op jit(solution)/shard_map/ppermute | solution.py:250
  117.0 16.6 %all-to-all-start.3 = ((f32[16,40,128]{2,1,0:T(8,128)}), f32[16,40,128]{2,1,0:T(8,128)S(1)}, u32[]{:S(2)}, u32[]{:S(2)}) async-start(f32[16,40,128]{2,1,0:T(8,128)} %bitcast.7), calls=%async_computation.3 | async-start | bytes 655360 | tf_op jit(solution)/shard_map/all_to_all | solution.py:241
  127.7 12.7 %collective-permute-start.11 = (f32[2,64,384]{2,1,0:T(8,128)}, f32[2,64,384]{2,1,0:T(8,128)S(1)}, u32[]{:S(2)}, u32[]{:S(2)}) collective-permute-start(f32[2,64,384]{2,1,0:T(8,128)} %get-tuple-element.17), channel_id=1, source_target_pairs={{0,32},{64,96},{128,160},{192,224},{32,0},{96,64},{160,128},{224,1... | collective-permute-start | bytes 589832 | tf_op jit(solution)/shard_map/ppermute | solution.py:207
  128.9 11.5 %collective-permute-start.12 = (f32[2,64,384]{2,1,0:T(8,128)S(1)}, f32[2,64,384]{2,1,0:T(8,128)S(1)}, u32[]{:S(2)}, u32[]{:S(2)}) collective-permute-start(f32[2,64,384]{2,1,0:T(8,128)S(1)} %get-tuple-element.16), channel_id=1, source_target_pairs={{96,128},{128,96},{97,129},{129,97},{98,130},{130,98},{99,131},{13... | collective-permute-start | bytes 589832 | tf_op jit(solution)/shard_map/ppermute | solution.py:207
  129.6 10.8 %collective-permute-start.13 = (f32[2,64,384]{2,1,0:T(8,128)S(1)}, f32[2,64,384]{2,1,0:T(8,128)S(1)}, u32[]{:S(2)}, u32[]{:S(2)}) collective-permute-start(f32[2,64,384]{2,1,0:T(8,128)S(1)} %get-tuple-element.16), channel_id=1, source_target_pairs={{32,64},{160,192},{64,32},{192,160},{33,65},{161,193},{65,33},{193... | collective-permute-start | bytes 589832 | tf_op jit(solution)/shard_map/ppermute | solution.py:207
  134.3 15.1 %all-to-all-start.4 = ((f32[8,40,128]{2,1,0:T(8,128)}), f32[8,40,128]{2,1,0:T(8,128)S(1)}, u32[]{:S(2)}, u32[]{:S(2)}) async-start(f32[8,40,128]{2,1,0:T(8,128)} %broadcast_in_dim.40), calls=%async_computation.4 | async-start | bytes 327680 | tf_op jit(solution)/shard_map/all_to_all | solution.py:241
  150.1 10.6 %all-to-all-start.5 = ((f32[16,40,128]{2,1,0:T(8,128)}), f32[16,40,128]{2,1,0:T(8,128)S(1)}, u32[]{:S(2)}, u32[]{:S(2)}) async-start(f32[16,40,128]{2,1,0:T(8,128)} %broadcast_in_dim.41), calls=%async_computation.5 | async-start | bytes 655360 | tf_op jit(solution)/shard_map/all_to_all | solution.py:241
  155.0 10.1 %collective-permute-start.14 = (f32[2,256,64]{2,1,0:T(8,128)S(1)}, f32[2,256,64]{2,1,0:T(8,128)S(1)}, u32[]{:S(2)}, u32[]{:S(2)}) collective-permute-start(f32[2,256,64]{2,1,0:T(8,128)S(1)} %get-tuple-element.24), channel_id=1, source_target_pairs={{0,1},{2,3},{4,5},{6,7},{8,9},{10,11},{12,13},{14,15},{16,17},{18,... | collective-permute-start | bytes 393224 | tf_op jit(solution)/shard_map/ppermute | solution.py:207
  158.6 9.8 %collective-permute-start.15 = (f32[2,256,64]{2,1,0:T(8,128)S(1)}, f32[2,256,64]{2,1,0:T(8,128)S(1)}, u32[]{:S(2)}, u32[]{:S(2)}) collective-permute-start(f32[2,256,64]{2,1,0:T(8,128)S(1)} %get-tuple-element.25), channel_id=1, source_target_pairs={{1,2},{3,4},{5,6},{7,8},{9,10},{11,12},{13,14},{15,16},{17,18},{19... | collective-permute-start | bytes 393224 | tf_op jit(solution)/shard_map/ppermute | solution.py:207
  160.7 9.9 %collective-permute-start.17 = (f32[640,128]{1,0:T(8,128)S(1)}, f32[640,128]{1,0:T(8,128)S(1)}, u32[]{:S(2)}, u32[]{:S(2)}) collective-permute-start(f32[640,128]{1,0:T(8,128)S(1)} %bitcast.19), channel_id=1, source_target_pairs={{0,1},{1,0},{2,3},{3,2},{4,5},{5,4},{6,7},{7,6},{8,9},{9,8},{10,11... | collective-permute-start | bytes 983048 | tf_op jit(solution)/shard_map/ppermute | solution.py:250
  (16 other events, 22.4 us)

commit v3 on v2

--- a/solution.py
+++ b/solution.py
@@ -199,22 +199,16 @@
     )(starts, count, core, *operands)
 
 
-def neighbours(low_strip, high_strip, axis, apart=False):
+def neighbours(low_strip, high_strip, axis):
     count = lax.axis_size(axis)
     odd = lax.axis_index(axis) % 2 == 1
 
-    def meet(block, pairs):
+    def meet(block, start):
+        pairs = [(i, i + 1) for i in range(start, count - 1, 2)]
         return lax.ppermute(block, axis, pairs + [(j, i) for i, j in pairs])
 
-    middle = [(count // 2 - 1, count // 2)]
-    pairs = [(i, i + 1) for i in range(1, count - 1, 2)]
-    block = jnp.where(odd, high_strip, low_strip)
-    first = meet(block, middle if apart else pairs)
-    if apart:
-        first = first + meet(block, [pair for pair in pairs if pair not in middle])
-    second = meet(
-        jnp.where(odd, low_strip, high_strip), [(i, i + 1) for i in range(0, count - 1, 2)]
-    )
+    first = meet(jnp.where(odd, high_strip, low_strip), 1)
+    second = meet(jnp.where(odd, low_strip, high_strip), 0)
     return jnp.where(odd, second, first), jnp.where(odd, first, second)
 
 
@@ -289,7 +283,7 @@
     updates, mine, other = run_pass(starts, count, core, frame, probe, None, amplitude, tables, margin)
     means = total(mine, other)
     strips = at(updates, 2, left, right)
-    low, high = neighbours(at(strips, 1, 0, 2 * rim), at(strips, 1, rows, tall), "row", True)
+    low, high = neighbours(at(strips, 1, 0, 2 * rim), at(strips, 1, rows, tall), "row")
     strips = strips + padded(low, 1, 0, tall) + padded(high, 1, rows, tall)
     low, high = neighbours(at(strips, 2, 0, 2 * rim), at(strips, 2, cols, cols + 2 * rim), "col")
     strips = strips + padded(low, 2, 0, cols + 2 * rim) + padded(high, 2, cols, cols + 2 * rim)
@@ -305,7 +299,7 @@
     )
     mine, other = total(mine, other)
     strips = at(updates, 2, left, right)
-    low, high = neighbours(at(strips, 1, 0, rim), at(strips, 1, tall - rim, tall), "row", True)
+    low, high = neighbours(at(strips, 1, 0, rim), at(strips, 1, tall - rim, tall), "row")
     middle = at(strips, 1, rim, rim + rows)
     middle = middle + padded(low, 1, 0, rows) + padded(high, 1, rows - rim, rows)
     low, high = neighbours(at(middle, 2, 0, rim), at(middle, 2, rim + cols, cols + 2 * rim), "col")

time: 173 us -> 172 us (level)
  waiting for transfers between devices: 36.8 us -> 39.1 us
  starting transfers between devices: 94.9 us -> 92.8 us
    all_to_all x6, waiting for transfers between devices: 20.1 us -> 22.5 us  [exchange(): lax.all_to_all(blocks, AXES, 0, 0, axis_index_groups=members, tiled=True)]
    ppermute x14 -> x12, starting transfers between devices: 30.8 us -> 28.5 us  [meet(): return lax.ppermute(block, axis, pairs + [(j, i) for i, j in pairs])]
    ppermute x14 -> x12, waiting for transfers between devices: 13.3 us -> 13.2 us  [meet(): return lax.ppermute(block, axis, pairs + [(j, i) for i, j in pairs])]
  transfers between devices with their start and end apart: 24 -> 22, of which waited for: 12 -> 12; matrix products, arithmetic and copies ran while one was open for 10% -> 10% of each run, Pallas kernels for 0% -> 0%
where the time goes in v3:
time: 172 us; the launch traced here: 171 us
  starting transfers between devices  92.8 us (54%)
  waiting for transfers between devices  39.1 us (23%)
  other arithmetic  20.7 us (12%)
  Pallas kernels  12.3 us (7%)
  local copies, waits for them, and re-layouts  4.41 us (3%)
  between operations  1.78 us (1%)
    all_to_all x6, starting transfers between devices, exchange(): lax.all_to_all(blocks, AXES, 0, 0, axis_index_groups=members, tiled=True)  56.6 us
    ppermute x12, starting transfers between devices, meet(): return lax.ppermute(block, axis, pairs + [(j, i) for i, j in pairs])  28.5 us
    all_to_all x6, waiting for transfers between devices, exchange(): lax.all_to_all(blocks, AXES, 0, 0, axis_index_groups=members, tiled=True)  22.5 us
    ppermute x12, waiting for transfers between devices, meet(): return lax.ppermute(block, axis, pairs + [(j, i) for i, j in pairs])  13.2 us
    pallas_call x2, Pallas kernels, run_pass(): pl.pallas_call(functools.partial(pass_kernel, modes=modes, size=size, mar...  12.3 us
    ppermute x4, starting transfers between devices, swap(): return lax.ppermute(block, 'col', [(i, i ^ 1) for i in range(count)])  7.75 us
    select_n x6, other arithmetic, neighbours(): second = meet(jnp.where(odd, low_strip, high_strip), 0)  4.55 us
  transfers between devices with their start and end apart: 22, of which 12 were waited for; matrix products, arithmetic and copies ran while one was open for 10% of the time, Pallas kernels for 0%

profile of v3, /device:TPU:25, one launch (start us, length us, event | category | flops | bytes accessed | tf_op | source)
XLA Modules:
  0.0 171.1 jit_solution(391728427629056863)
XLA Ops:
  3.6 2.5 %collective-permute-done = f32[2,64,256]{2,1,0:T(8,128)S(1)} collective-permute-done((f32[2,64,256]{2,1,0:T(8,128)S(1)}, f32[2,64,256]{2,1,0:T(8,128)S(1)}, u32[]{:S(2)}, u32[]{:S(2)}) %collective-permute-start) | collective-permute-done | bytes 131104 | tf_op jit(solution)/shard_map/ppermute | solution.py:208
  7.5 1.6 collective-permute-start.2
  9.1 3.2 %collective-permute-start.3 = (f32[2,384,128]{2,1,0:T(8,128)S(1)}, f32[2,384,128]{2,1,0:T(8,128)S(1)}, u32[]{:S(2)}, u32[]{:S(2)}) collective-permute-start(f32[2,384,128]{2,1,0:T(8,128)S(1)} %get-tuple-element.31), channel_id=1, source_target_pairs={{1,2},{3,4},{5,6},{7,8},{9,10},{11,12},{13,14},{15,16},{17,18},{19... | collective-permute-start | bytes 1179656 | tf_op jit(solution)/shard_map/ppermute | solution.py:208
  13.3 7.0 %collective-permute-done.3 = f32[2,384,128]{2,1,0:T(8,128)S(1)} collective-permute-done((f32[2,384,128]{2,1,0:T(8,128)S(1)}, f32[2,384,128]{2,1,0:T(8,128)S(1)}, u32[]{:S(2)}, u32[]{:S(2)}) %collective-permute-start.3) | collective-permute-done | bytes 393248 | tf_op jit(solution)/shard_map/ppermute | solution.py:208
  21.8 5.6 %shard_map.113 = (f32[2,384,512]{2,1,0:T(8,128)S(1)}, f32[640,128]{1,0:T(8,128)S(1)}, f32[640,128]{1,0:T(8,128)S(1)}) custom-call(s32[8,2]{1,0:T(8,128)S(1)} %copy.14.refs_0_, s32[1]{0:T(128)} %bitcast.14.refs_1_, s32[1]{0:T(128)} %bitcast.2.refs_2_, f32[2,384,512]{2,1,0:T(8,128)S(1)} %pad_maximum_fusion.refs_3_, f32[2,4,128,128]{3,2,1,0:T(8,128)S(1)} %copy-done, ...), custom_call_target="tpu_custom_call" | custom-call | flops 6442450944 | bytes 6291456 | tf_op jit(solution)/shard_map/pallas_call | solution.py:191
  28.6 8.3 %collective-permute-start.4 = (f32[2,128,384]{2,1,0:T(8,128)}, f32[2,128,384]{2,1,0:T(8,128)}, u32[]{:S(2)}, u32[]{:S(2)}) collective-permute-start(f32[2,128,384]{2,1,0:T(8,128)} %get-tuple-element.18), channel_id=1, source_target_pairs={{0,32},{64,96},{128,160},{192,224},{32,0},{96,64},{160,128},{224,1... | collective-permute-start | bytes 1179656 | tf_op jit(solution)/shard_map/ppermute | solution.py:208
  38.4 1.8 %collective-permute-done.8 = f32[640,128]{1,0:T(8,128)} collective-permute-done((f32[640,128]{1,0:T(8,128)S(1)}, f32[640,128]{1,0:T(8,128)}, u32[]{:S(2)}, u32[]{:S(2)}) %collective-permute-start.8) | collective-permute-done | bytes 327712 | tf_op jit(solution)/shard_map/ppermute | solution.py:244
  40.1 1.8 %add.107 = f32[640,128]{1,0:T(8,128)} add(f32[640,128]{1,0:T(8,128)S(1)} %get-tuple-element.10, f32[640,128]{1,0:T(8,128)} %collective-permute-done.8) | non-fusion elementwise | flops 81920 | bytes 983040 | tf_op jit(solution)/shard_map/add | solution.py:249
  41.9 19.0 %all-to-all-start = ((f32[16,40,128]{2,1,0:T(8,128)}), f32[16,40,128]{2,1,0:T(8,128)S(1)}, u32[]{:S(2)}, u32[]{:S(2)}) async-start(f32[16,40,128]{2,1,0:T(8,128)} %bitcast.5), calls=%async_computation | async-start | bytes 655360 | tf_op jit(solution)/shard_map/all_to_all | solution.py:235
  62.1 1.5 pad_add_fusion.1
  63.6 4.0 %all-to-all-done = f32[16,40,128]{2,1,0:T(8,128)S(1)} async-done(((f32[16,40,128]{2,1,0:T(8,128)}), f32[16,40,128]{2,1,0:T(8,128)S(1)}, u32[]{:S(2)}, u32[]{:S(2)}) %all-to-all-start) | async-done | bytes 327712 | tf_op jit(solution)/shard_map/all_to_all | solution.py:235
  68.2 13.5 %all-to-all-start.1 = ((f32[8,40,128]{2,1,0:T(8,128)}), f32[8,40,128]{2,1,0:T(8,128)S(1)}, u32[]{:S(2)}, u32[]{:S(2)}) async-start(f32[8,40,128]{2,1,0:T(8,128)} %broadcast_in_dim.22), calls=%async_computation.1 | async-start | bytes 327680 | tf_op jit(solution)/shard_map/all_to_all | solution.py:235
  81.8 2.0 %slice_select_fusion.1 = (f32[2,384,128]{2,1,0:T(8,128)}, f32[2,384,128]{2,1,0:T(8,128)}) fusion(f32[2,384,384]{2,1,0:T(8,128)} %pad_add_fusion.1, pred[]{:T(512)S(6)} %eq.22), kind=kLoop, calls=%fused_computation.14 | loop fusion | flops 196608 | bytes 1572865 | tf_op jit(solution)/shard_map/jit(_where)/select_n | solution.py:211
  84.7 4.0 %collective-permute-start.7 = (f32[2,384,128]{2,1,0:T(8,128)}, f32[2,384,128]{2,1,0:T(8,128)}, u32[]{:S(2)}, u32[]{:S(2)}) collective-permute-start(f32[2,384,128]{2,1,0:T(8,128)} %get-tuple-element.21), channel_id=1, source_target_pairs={{1,2},{3,4},{5,6},{7,8},{9,10},{11,12},{13,14},{15,16},{17,18},{19... | collective-permute-start | bytes 1179656 | tf_op jit(solution)/shard_map/ppermute | solution.py:208
  88.7 1.4 all-to-all-done.1
  90.9 4.0 %all-to-all-start.2 = ((f32[16,40,128]{2,1,0:T(8,128)}), f32[16,40,128]{2,1,0:T(8,128)S(1)}, u32[]{:S(2)}, u32[]{:S(2)}) async-start(f32[16,40,128]{2,1,0:T(8,128)} %broadcast_in_dim.23), calls=%async_computation.2 | async-start | bytes 655360 | tf_op jit(solution)/shard_map/all_to_all | solution.py:235
  96.2 1.9 %broadcast_select_fusion.3 = (f32[2,384,128]{2,1,0:T(8,128)}, f32[2,384,128]{2,1,0:T(8,128)}) fusion(f32[2,384,128]{2,1,0:T(8,128)S(1)} %collective-permute-done.6, f32[2,384,128]{2,1,0:T(8,128)} %collective-permute-done.7, pred[]{:T(512)S(6)} %eq.22), kind=kLoop, calls=%fused_computation.24 | loop fusion | flops 196608 | bytes 1572865 | tf_op jit(solution)/shard_map/jit(_where)/select_n | solution.py:212
  98.1 2.7 %all-to-all-done.2 = f32[16,40,128]{2,1,0:T(8,128)S(1)} async-done(((f32[16,40,128]{2,1,0:T(8,128)}), f32[16,40,128]{2,1,0:T(8,128)S(1)}, u32[]{:S(2)}, u32[]{:S(2)}) %all-to-all-start.2) | async-done | bytes 327712 | tf_op jit(solution)/shard_map/all_to_all | solution.py:235
  100.9 3.6 %collective-permute-start.9 = (f32[640,128]{1,0:T(8,128)S(1)}, f32[640,128]{1,0:T(8,128)S(1)}, u32[]{:S(2)}, u32[]{:S(2)}) collective-permute-start(f32[640,128]{1,0:T(8,128)S(1)} %bitcast.16), channel_id=1, source_target_pairs={{0,1},{1,0},{2,3},{3,2},{4,5},{5,4},{6,7},{7,6},{8,9},{9,8},{10,11... | collective-permute-start | bytes 983048 | tf_op jit(solution)/shard_map/ppermute | solution.py:244
  106.1 1.7 select_add_fusion.refs_3_
  107.8 6.7 %shard_map.114 = (f32[2,384,512]{2,1,0:T(8,128)S(1)}, f32[640,128]{1,0:T(8,128)S(1)}, f32[640,128]{1,0:T(8,128)S(1)}, f32[2,4,128,128]{3,2,1,0:T(8,128)S(1)}) custom-call(s32[8,2]{1,0:T(8,128)S(1)} %copy.14.refs_0_, s32[1]{0:T(128)} %bitcast.15.refs_1_, s32[1]{0:T(128)} %bitcast.2.refs_2_, f32[2,384,512]{2,1,0:T(8,128)} %select_add_fusion.refs_3_, ...), custom_call_target="tpu_custom_call" | custom-call | flops 6442450944 | bytes 6291456 | tf_op jit(solution)/shard_map/pallas_call | solution.py:191
  114.7 1.6 collective-permute-done.14
  117.0 9.9 %all-to-all-start.3 = ((f32[16,40,128]{2,1,0:T(8,128)}), f32[16,40,128]{2,1,0:T(8,128)S(1)}, u32[]{:S(2)}, u32[]{:S(2)}) async-start(f32[16,40,128]{2,1,0:T(8,128)} %bitcast.7), calls=%async_computation.3 | async-start | bytes 655360 | tf_op jit(solution)/shard_map/all_to_all | solution.py:235
  129.1 4.6 %all-to-all-done.3 = f32[16,40,128]{2,1,0:T(8,128)S(1)} async-done(((f32[16,40,128]{2,1,0:T(8,128)}), f32[16,40,128]{2,1,0:T(8,128)S(1)}, u32[]{:S(2)}, u32[]{:S(2)}) %all-to-all-start.3) | async-done | bytes 327712 | tf_op jit(solution)/shard_map/all_to_all | solution.py:235
  134.4 4.8 %all-to-all-start.4 = ((f32[8,40,128]{2,1,0:T(8,128)}), f32[8,40,128]{2,1,0:T(8,128)S(1)}, u32[]{:S(2)}, u32[]{:S(2)}) async-start(f32[8,40,128]{2,1,0:T(8,128)} %broadcast_in_dim.40), calls=%async_computation.4 | async-start | bytes 327680 | tf_op jit(solution)/shard_map/all_to_all | solution.py:235
  139.5 9.2 %all-to-all-done.4 = f32[8,40,128]{2,1,0:T(8,128)S(1)} async-done(((f32[8,40,128]{2,1,0:T(8,128)}), f32[8,40,128]{2,1,0:T(8,128)S(1)}, u32[]{:S(2)}, u32[]{:S(2)}) %all-to-all-start.4) | async-done | bytes 163872 | tf_op jit(solution)/shard_map/all_to_all | solution.py:235
  149.5 5.3 %all-to-all-start.5 = ((f32[16,40,128]{2,1,0:T(8,128)}), f32[16,40,128]{2,1,0:T(8,128)S(1)}, u32[]{:S(2)}, u32[]{:S(2)}) async-start(f32[16,40,128]{2,1,0:T(8,128)} %broadcast_in_dim.41), calls=%async_computation.5 | async-start | bytes 655360 | tf_op jit(solution)/shard_map/all_to_all | solution.py:235
  154.9 3.3 %collective-permute-start.12 = (f32[2,256,64]{2,1,0:T(8,128)S(1)}, f32[2,256,64]{2,1,0:T(8,128)S(1)}, u32[]{:S(2)}, u32[]{:S(2)}) collective-permute-start(f32[2,256,64]{2,1,0:T(8,128)S(1)} %get-tuple-element.22), channel_id=1, source_target_pairs={{0,1},{2,3},{4,5},{6,7},{8,9},{10,11},{12,13},{14,15},{16,17},{18,... | collective-permute-start | bytes 393224 | tf_op jit(solution)/shard_map/ppermute | solution.py:208
  158.2 1.9 %collective-permute-start.13 = (f32[2,256,64]{2,1,0:T(8,128)S(1)}, f32[2,256,64]{2,1,0:T(8,128)S(1)}, u32[]{:S(2)}, u32[]{:S(2)}) collective-permute-start(f32[2,256,64]{2,1,0:T(8,128)S(1)} %get-tuple-element.23), channel_id=1, source_target_pairs={{1,2},{3,4},{5,6},{7,8},{9,10},{11,12},{13,14},{15,16},{17,18},{19... | collective-permute-start | bytes 393224 | tf_op jit(solution)/shard_map/ppermute | solution.py:208
  160.6 4.0 %collective-permute-start.15 = (f32[640,128]{1,0:T(8,128)S(1)}, f32[640,128]{1,0:T(8,128)S(1)}, u32[]{:S(2)}, u32[]{:S(2)}) collective-permute-start(f32[640,128]{1,0:T(8,128)S(1)} %bitcast.19), channel_id=1, source_target_pairs={{0,1},{1,0},{2,3},{3,2},{4,5},{5,4},{6,7},{7,6},{8,9},{9,8},{10,11... | collective-permute-start | bytes 983048 | tf_op jit(solution)/shard_map/ppermute | solution.py:244
  164.6 3.3 %collective-permute-done.13 = f32[2,256,64]{2,1,0:T(8,128)S(1)} collective-permute-done((f32[2,256,64]{2,1,0:T(8,128)S(1)}, f32[2,256,64]{2,1,0:T(8,128)S(1)}, u32[]{:S(2)}, u32[]{:S(2)}) %collective-permute-start.13) | collective-permute-done | bytes 131104 | tf_op jit(solution)/shard_map/ppermute | solution.py:208
  168.0 2.1 %fusion.1 = f32[2,256,256]{2,1,0:T(8,128)} fusion(f32[2,256,384]{2,1,0:T(8,128)S(1)} %pad_add_fusion.2, f32[2,384,512]{2,1,0:T(8,128)} %select_add_fusion.refs_3_, f32[2,256,64]{2,1,0:T(8,128)S(1)} %get-tuple-element.35, f32[2,256,64]{2,1,0:T(8,128)S(1)} %get-tuple-element.34), kind=kLoop, calls=%fused_computation.10 | loop fusion | flops 393216 | bytes 1835008 | tf_op jit(solution)/shard_map/add | solution.py:308
  (100 shorter events, 21.4 us)
Async XLA Ops:
  1.6 4.5 %collective-permute-start = (f32[2,64,256]{2,1,0:T(8,128)S(1)}, f32[2,64,256]{2,1,0:T(8,128)S(1)}, u32[]{:S(2)}, u32[]{:S(2)}) collective-permute-start(f32[2,64,256]{2,1,0:T(8,128)S(1)} %get-tuple-element.36), channel_id=1, source_target_pairs={{0,32},{64,96},{128,160},{192,224},{32,0},{96,64},{160,128},{224,1... | collective-permute-start | bytes 393224 | tf_op jit(solution)/shard_map/ppermute | solution.py:208
  2.9 3.2 %collective-permute-start.1 = (f32[2,64,256]{2,1,0:T(8,128)S(1)}, f32[2,64,256]{2,1,0:T(8,128)S(1)}, u32[]{:S(2)}, u32[]{:S(2)}) collective-permute-start(f32[2,64,256]{2,1,0:T(8,128)S(1)} %get-tuple-element.37), channel_id=1, source_target_pairs={{32,64},{96,128},{160,192},{64,32},{128,96},{192,160},{33,65},{97,... | collective-permute-start | bytes 393224 | tf_op jit(solution)/shard_map/ppermute | solution.py:208
  6.1 14.2 %copy-start.16 = (f32[2,64,256]{2,1,0:T(8,128)}, f32[2,64,256]{2,1,0:T(8,128)S(1)}, u32[]{:S(2)}) copy-start(f32[2,64,256]{2,1,0:T(8,128)S(1)} %get-tuple-element.40) | copy-start | bytes 393220
  6.2 14.2 %copy-start.18 = (f32[2,64,256]{2,1,0:T(8,128)}, f32[2,64,256]{2,1,0:T(8,128)S(1)}, u32[]{:S(2)}) copy-start(f32[2,64,256]{2,1,0:T(8,128)S(1)} %get-tuple-element.41) | copy-start | bytes 393220
  6.2 6.2 %copy-start.23 = (s32[1,1,8,2]{2,3,1,0:T(2,128)S(1)}, s32[1,1,8,2]{2,3,1,0:T(2,128)}, u32[]{:S(2)}) copy-start(s32[1,1,8,2]{2,3,1,0:T(2,128)} %param.14) | copy-start | bytes 196
  6.2 6.9 %copy-start.21 = (bf16[1,1,8,128,128]{4,3,2,1,0:T(8,128)(2,1)S(1)}, bf16[1,1,8,128,128]{4,3,2,1,0:T(8,128)(2,1)}, u32[]{:S(2)}) copy-start(bf16[1,1,8,128,128]{4,3,2,1,0:T(8,128)(2,1)} %param.12) | copy-start | bytes 786436
  6.2 6.9 %copy-start.22 = (f32[1,1,8,128]{3,2,1,0:T(8,128)S(1)}, f32[1,1,8,128]{3,2,1,0:T(8,128)}, u32[]{:S(2)}) copy-start(f32[1,1,8,128]{3,2,1,0:T(8,128)} %param.13) | copy-start | bytes 12292
  7.5 12.9 %copy-start.10 = (f32[2,256,256]{2,1,0:T(8,128)S(1)}, f32[2,256,256]{2,1,0:T(8,128)}, u32[]{:S(2)}) copy-start(f32[2,256,256]{2,1,0:T(8,128)} %param.10) | copy-start | bytes 1572868
  7.5 5.8 %collective-permute-start.2 = (f32[2,384,128]{2,1,0:T(8,128)S(1)}, f32[2,384,128]{2,1,0:T(8,128)S(1)}, u32[]{:S(2)}, u32[]{:S(2)}) collective-permute-start(f32[2,384,128]{2,1,0:T(8,128)S(1)} %get-tuple-element.30), channel_id=1, source_target_pairs={{0,1},{2,3},{4,5},{6,7},{8,9},{10,11},{12,13},{14,15},{16,17},{18,... | collective-permute-start | bytes 1179656 | tf_op jit(solution)/shard_map/ppermute | solution.py:208
  9.1 11.2 %collective-permute-start.3 = (f32[2,384,128]{2,1,0:T(8,128)S(1)}, f32[2,384,128]{2,1,0:T(8,128)S(1)}, u32[]{:S(2)}, u32[]{:S(2)}) collective-permute-start(f32[2,384,128]{2,1,0:T(8,128)S(1)} %get-tuple-element.31), channel_id=1, source_target_pairs={{1,2},{3,4},{5,6},{7,8},{9,10},{11,12},{13,14},{15,16},{17,18},{19... | collective-permute-start | bytes 1179656 | tf_op jit(solution)/shard_map/ppermute | solution.py:208
  28.6 32.3 %collective-permute-start.4 = (f32[2,128,384]{2,1,0:T(8,128)}, f32[2,128,384]{2,1,0:T(8,128)}, u32[]{:S(2)}, u32[]{:S(2)}) collective-permute-start(f32[2,128,384]{2,1,0:T(8,128)} %get-tuple-element.18), channel_id=1, source_target_pairs={{0,32},{64,96},{128,160},{192,224},{32,0},{96,64},{160,128},{224,1... | collective-permute-start | bytes 1179656 | tf_op jit(solution)/shard_map/ppermute | solution.py:208
  37.0 23.9 %collective-permute-start.5 = (f32[2,128,384]{2,1,0:T(8,128)}, f32[2,128,384]{2,1,0:T(8,128)}, u32[]{:S(2)}, u32[]{:S(2)}) collective-permute-start(f32[2,128,384]{2,1,0:T(8,128)} %get-tuple-element.19), channel_id=1, source_target_pairs={{32,64},{96,128},{160,192},{64,32},{128,96},{192,160},{33,65},{97,... | collective-permute-start | bytes 1179656 | tf_op jit(solution)/shard_map/ppermute | solution.py:208
  38.4 1.8 %collective-permute-start.8 = (f32[640,128]{1,0:T(8,128)S(1)}, f32[640,128]{1,0:T(8,128)}, u32[]{:S(2)}, u32[]{:S(2)}) collective-permute-start(f32[640,128]{1,0:T(8,128)S(1)} %get-tuple-element.11), channel_id=1, source_target_pairs={{0,1},{1,0},{2,3},{3,2},{4,5},{5,4},{6,7},{7,6},{8,9},{9,8},{10,11... | collective-permute-start | bytes 983048 | tf_op jit(solution)/shard_map/ppermute | solution.py:244
  41.9 25.6 %all-to-all-start = ((f32[16,40,128]{2,1,0:T(8,128)}), f32[16,40,128]{2,1,0:T(8,128)S(1)}, u32[]{:S(2)}, u32[]{:S(2)}) async-start(f32[16,40,128]{2,1,0:T(8,128)} %bitcast.5), calls=%async_computation | async-start | bytes 655360 | tf_op jit(solution)/shard_map/all_to_all | solution.py:235
  68.2 21.9 %all-to-all-start.1 = ((f32[8,40,128]{2,1,0:T(8,128)}), f32[8,40,128]{2,1,0:T(8,128)S(1)}, u32[]{:S(2)}, u32[]{:S(2)}) async-start(f32[8,40,128]{2,1,0:T(8,128)} %broadcast_in_dim.22), calls=%async_computation.1 | async-start | bytes 327680 | tf_op jit(solution)/shard_map/all_to_all | solution.py:235
  83.8 20.7 %copy-start.9 = (f32[2,384,384]{2,1,0:T(8,128)S(1)}, f32[2,384,384]{2,1,0:T(8,128)}, u32[]{:S(2)}) copy-start(f32[2,384,384]{2,1,0:T(8,128)} %pad_add_fusion.1) | copy-start | bytes 3538948
  83.8 12.0 %collective-permute-start.6 = (f32[2,384,128]{2,1,0:T(8,128)}, f32[2,384,128]{2,1,0:T(8,128)S(1)}, u32[]{:S(2)}, u32[]{:S(2)}) collective-permute-start(f32[2,384,128]{2,1,0:T(8,128)} %get-tuple-element.20), channel_id=1, source_target_pairs={{0,1},{2,3},{4,5},{6,7},{8,9},{10,11},{12,13},{14,15},{16,17},{18,... | collective-permute-start | bytes 1179656 | tf_op jit(solution)/shard_map/ppermute | solution.py:208
  84.7 11.5 %collective-permute-start.7 = (f32[2,384,128]{2,1,0:T(8,128)}, f32[2,384,128]{2,1,0:T(8,128)}, u32[]{:S(2)}, u32[]{:S(2)}) collective-permute-start(f32[2,384,128]{2,1,0:T(8,128)} %get-tuple-element.21), channel_id=1, source_target_pairs={{1,2},{3,4},{5,6},{7,8},{9,10},{11,12},{13,14},{15,16},{17,18},{19... | collective-permute-start | bytes 1179656 | tf_op jit(solution)/shard_map/ppermute | solution.py:208
  90.9 9.9 %all-to-all-start.2 = ((f32[16,40,128]{2,1,0:T(8,128)}), f32[16,40,128]{2,1,0:T(8,128)S(1)}, u32[]{:S(2)}, u32[]{:S(2)}) async-start(f32[16,40,128]{2,1,0:T(8,128)} %broadcast_in_dim.23), calls=%async_computation.2 | async-start | bytes 655360 | tf_op jit(solution)/shard_map/all_to_all | solution.py:235
  100.9 6.9 %collective-permute-start.9 = (f32[640,128]{1,0:T(8,128)S(1)}, f32[640,128]{1,0:T(8,128)S(1)}, u32[]{:S(2)}, u32[]{:S(2)}) collective-permute-start(f32[640,128]{1,0:T(8,128)S(1)} %bitcast.16), channel_id=1, source_target_pairs={{0,1},{1,0},{2,3},{3,2},{4,5},{5,4},{6,7},{7,6},{8,9},{9,8},{10,11... | collective-permute-start | bytes 983048 | tf_op jit(solution)/shard_map/ppermute | solution.py:244
  106.1 1.7 copy-start.4
  106.1 1.7 copy-start.6
  106.1 1.7 copy-start.8
  114.6 1.7 %collective-permute-start.14 = (f32[640,128]{1,0:T(8,128)S(1)}, f32[640,128]{1,0:T(8,128)S(1)}, u32[]{:S(2)}, u32[]{:S(2)}) collective-permute-start(f32[640,128]{1,0:T(8,128)S(1)} %get-tuple-element.15), channel_id=1, source_target_pairs={{0,1},{1,0},{2,3},{3,2},{4,5},{5,4},{6,7},{7,6},{8,9},{9,8},{10,11... | collective-permute-start | bytes 983048 | tf_op jit(solution)/shard_map/ppermute | solution.py:244
  117.0 16.6 %all-to-all-start.3 = ((f32[16,40,128]{2,1,0:T(8,128)}), f32[16,40,128]{2,1,0:T(8,128)S(1)}, u32[]{:S(2)}, u32[]{:S(2)}) async-start(f32[16,40,128]{2,1,0:T(8,128)} %bitcast.7), calls=%async_computation.3 | async-start | bytes 655360 | tf_op jit(solution)/shard_map/all_to_all | solution.py:235
  127.1 12.1 %collective-permute-start.10 = (f32[2,64,384]{2,1,0:T(8,128)S(1)}, f32[2,64,384]{2,1,0:T(8,128)S(1)}, u32[]{:S(2)}, u32[]{:S(2)}) collective-permute-start(f32[2,64,384]{2,1,0:T(8,128)S(1)} %get-tuple-element.16), channel_id=1, source_target_pairs={{0,32},{64,96},{128,160},{192,224},{32,0},{96,64},{160,128},{224,1... | collective-permute-start | bytes 589832 | tf_op jit(solution)/shard_map/ppermute | solution.py:208
  128.4 10.8 %collective-permute-start.11 = (f32[2,64,384]{2,1,0:T(8,128)S(1)}, f32[2,64,384]{2,1,0:T(8,128)S(1)}, u32[]{:S(2)}, u32[]{:S(2)}) collective-permute-start(f32[2,64,384]{2,1,0:T(8,128)S(1)} %get-tuple-element.17), channel_id=1, source_target_pairs={{32,64},{96,128},{160,192},{64,32},{128,96},{192,160},{33,65},{97,... | collective-permute-start | bytes 589832 | tf_op jit(solution)/shard_map/ppermute | solution.py:208
  134.4 14.4 %all-to-all-start.4 = ((f32[8,40,128]{2,1,0:T(8,128)}), f32[8,40,128]{2,1,0:T(8,128)S(1)}, u32[]{:S(2)}, u32[]{:S(2)}) async-start(f32[8,40,128]{2,1,0:T(8,128)} %broadcast_in_dim.40), calls=%async_computation.4 | async-start | bytes 327680 | tf_op jit(solution)/shard_map/all_to_all | solution.py:235
  149.5 11.1 %all-to-all-start.5 = ((f32[16,40,128]{2,1,0:T(8,128)}), f32[16,40,128]{2,1,0:T(8,128)S(1)}, u32[]{:S(2)}, u32[]{:S(2)}) async-start(f32[16,40,128]{2,1,0:T(8,128)} %broadcast_in_dim.41), calls=%async_computation.5 | async-start | bytes 655360 | tf_op jit(solution)/shard_map/all_to_all | solution.py:235
  154.9 9.7 %collective-permute-start.12 = (f32[2,256,64]{2,1,0:T(8,128)S(1)}, f32[2,256,64]{2,1,0:T(8,128)S(1)}, u32[]{:S(2)}, u32[]{:S(2)}) collective-permute-start(f32[2,256,64]{2,1,0:T(8,128)S(1)} %get-tuple-element.22), channel_id=1, source_target_pairs={{0,1},{2,3},{4,5},{6,7},{8,9},{10,11},{12,13},{14,15},{16,17},{18,... | collective-permute-start | bytes 393224 | tf_op jit(solution)/shard_map/ppermute | solution.py:208
  158.2 9.8 %collective-permute-start.13 = (f32[2,256,64]{2,1,0:T(8,128)S(1)}, f32[2,256,64]{2,1,0:T(8,128)S(1)}, u32[]{:S(2)}, u32[]{:S(2)}) collective-permute-start(f32[2,256,64]{2,1,0:T(8,128)S(1)} %get-tuple-element.23), channel_id=1, source_target_pairs={{1,2},{3,4},{5,6},{7,8},{9,10},{11,12},{13,14},{15,16},{17,18},{19... | collective-permute-start | bytes 393224 | tf_op jit(solution)/shard_map/ppermute | solution.py:208
  160.6 9.5 %collective-permute-start.15 = (f32[640,128]{1,0:T(8,128)S(1)}, f32[640,128]{1,0:T(8,128)S(1)}, u32[]{:S(2)}, u32[]{:S(2)}) collective-permute-start(f32[640,128]{1,0:T(8,128)S(1)} %bitcast.19), channel_id=1, source_target_pairs={{0,1},{1,0},{2,3},{3,2},{4,5},{5,4},{6,7},{7,6},{8,9},{9,8},{10,11... | collective-permute-start | bytes 983048 | tf_op jit(solution)/shard_map/ppermute | solution.py:244
  (14 other events, 19.1 us)

commit v4 on v3

--- a/solution.py
+++ b/solution.py
@@ -286,13 +286,14 @@
     low, high = neighbours(at(strips, 1, 0, 2 * rim), at(strips, 1, rows, tall), "row")
     strips = strips + padded(low, 1, 0, tall) + padded(high, 1, rows, tall)
     low, high = neighbours(at(strips, 2, 0, 2 * rim), at(strips, 2, cols, cols + 2 * rim), "col")
-    strips = strips + padded(low, 2, 0, cols + 2 * rim) + padded(high, 2, cols, cols + 2 * rim)
-    updates = padded(strips, 2, left, wide)
     at_row = lax.broadcasted_iota(jnp.int32, (1, tall, 1), 1) + (lax.axis_index("row") * rows - rim)
     at_col = lax.broadcasted_iota(jnp.int32, (1, 1, wide), 2) + (lax.axis_index("col") * cols - LANES)
     inside = (at_row >= 0) & (at_row < rows * lax.axis_size("row"))
     inside = inside & (at_col >= 0) & (at_col < cols * lax.axis_size("col"))
-    frame = frame + jnp.where(inside, updates, 0.0)
+    early = frame + jnp.where(inside, padded(strips, 2, left, wide), 0.0)
+    early, low, high = lax.optimization_barrier((early, low, high))
+    late = padded(low, 2, left, wide) + padded(high, 2, left + cols, wide)
+    frame = early + jnp.where(inside, late, 0.0)
 
     updates, mine, other, probe = run_pass(
         starts, count, core, frame, probe, means, amplitude, tables, margin

time: 172 us -> 175 us (1.017)
    all_to_all x6, starting transfers between devices: 56.6 us -> 59.7 us  [exchange(): lax.all_to_all(blocks, AXES, 0, 0, axis_index_groups=members, tiled=True)]
    add x2, other arithmetic: 3.05 us -> 5.42 us  [the longest x1 2.76 us: on_device(): early = frame + jnp.where(inside, padded(strips, 2, left, wide), 0.0)]
    select_n x6 -> x5, other arithmetic: 4.55 us -> 2.5 us  [neighbours(): second = meet(jnp.where(odd, low_strip, high_strip), 0)]
    reduce_sum x4, other arithmetic: 0.08 us -> 1.97 us  [total(): part = jnp.sum(spread(jnp.sum(parts, axis=0), lines), axis=0)]
    ppermute x4, waiting for transfers between devices: 3.38 us -> 1.62 us  [swap(): return lax.ppermute(block, 'col', [(i, i ^ 1) for i in range(count)])]
  transfers between devices with their start and end apart: 22 -> 22, of which waited for: 12 -> 10; matrix products, arithmetic and copies ran while one was open for 10% -> 10% of each run, Pallas kernels for 0% -> 0%
where the time goes in v4:
time: 175 us; the launch traced here: 174 us
  starting transfers between devices  94 us (54%)
  waiting for transfers between devices  38.5 us (22%)
  other arithmetic  21.3 us (12%)
  Pallas kernels  12.2 us (7%)
  local copies, waits for them, and re-layouts  5.96 us (3%)
  between operations  1.8 us (1%)
    all_to_all x6, starting transfers between devices, exchange(): lax.all_to_all(blocks, AXES, 0, 0, axis_index_groups=members, tiled=True)  59.7 us
    ppermute x12, starting transfers between devices, meet(): return lax.ppermute(block, axis, pairs + [(j, i) for i, j in pairs])  27.6 us
    all_to_all x6, waiting for transfers between devices, exchange(): lax.all_to_all(blocks, AXES, 0, 0, axis_index_groups=members, tiled=True)  24 us
    ppermute x12, waiting for transfers between devices, meet(): return lax.ppermute(block, axis, pairs + [(j, i) for i, j in pairs])  12.8 us
    pallas_call x2, Pallas kernels, run_pass(): pl.pallas_call(functools.partial(pass_kernel, modes=modes, size=size, mar...  12.2 us
    ppermute x4, starting transfers between devices, swap(): return lax.ppermute(block, 'col', [(i, i ^ 1) for i in range(count)])  6.72 us
  transfers between devices with their start and end apart: 22, of which 10 were waited for; matrix products, arithmetic and copies ran while one was open for 10% of the time, Pallas kernels for 0%

profile of v4, /device:TPU:25, one launch (start us, length us, event | category | flops | bytes accessed | tf_op | source)
XLA Modules:
  0.0 173.7 jit_solution(8193223267246391571)
XLA Ops:
  1.6 1.3 collective-permute-start
  3.6 2.5 %collective-permute-done = f32[2,64,256]{2,1,0:T(8,128)S(1)} collective-permute-done((f32[2,64,256]{2,1,0:T(8,128)S(1)}, f32[2,64,256]{2,1,0:T(8,128)S(1)}, u32[]{:S(2)}, u32[]{:S(2)}) %collective-permute-start) | collective-permute-done | bytes 131104 | tf_op jit(solution)/shard_map/ppermute | solution.py:208
  7.5 1.6 collective-permute-start.2
  9.1 3.2 %collective-permute-start.3 = (f32[2,384,128]{2,1,0:T(8,128)S(1)}, f32[2,384,128]{2,1,0:T(8,128)S(1)}, u32[]{:S(2)}, u32[]{:S(2)}) collective-permute-start(f32[2,384,128]{2,1,0:T(8,128)S(1)} %get-tuple-element.37), channel_id=1, source_target_pairs={{1,2},{3,4},{5,6},{7,8},{9,10},{11,12},{13,14},{15,16},{17,18},{19... | collective-permute-start | bytes 1179656 | tf_op jit(solution)/shard_map/ppermute | solution.py:208
  13.3 7.0 %collective-permute-done.3 = f32[2,384,128]{2,1,0:T(8,128)S(1)} collective-permute-done((f32[2,384,128]{2,1,0:T(8,128)S(1)}, f32[2,384,128]{2,1,0:T(8,128)S(1)}, u32[]{:S(2)}, u32[]{:S(2)}) %collective-permute-start.3) | collective-permute-done | bytes 393248 | tf_op jit(solution)/shard_map/ppermute | solution.py:208
  21.8 5.6 %shard_map.113 = (f32[2,384,512]{2,1,0:T(8,128)S(1)}, f32[640,128]{1,0:T(8,128)S(1)}, f32[640,128]{1,0:T(8,128)S(1)}) custom-call(s32[8,2]{1,0:T(8,128)S(1)} %copy.14.refs_0_, s32[1]{0:T(128)} %bitcast.14.refs_1_, s32[1]{0:T(128)} %bitcast.2.refs_2_, f32[2,384,512]{2,1,0:T(8,128)S(1)} %pad_maximum_fusion.refs_3_, f32[2,4,128,128]{3,2,1,0:T(8,128)S(1)} %copy-done, ...), custom_call_target="tpu_custom_call" | custom-call | flops 6442450944 | bytes 6291456 | tf_op jit(solution)/shard_map/pallas_call | solution.py:191
  28.7 8.3 %collective-permute-start.4 = (f32[2,128,384]{2,1,0:T(8,128)}, f32[2,128,384]{2,1,0:T(8,128)}, u32[]{:S(2)}, u32[]{:S(2)}) collective-permute-start(f32[2,128,384]{2,1,0:T(8,128)} %get-tuple-element.24), channel_id=1, source_target_pairs={{0,32},{64,96},{128,160},{192,224},{32,0},{96,64},{160,128},{224,1... | collective-permute-start | bytes 1179656 | tf_op jit(solution)/shard_map/ppermute | solution.py:208
  37.1 1.4 collective-permute-start.5
  38.5 1.7 add.107
  40.2 18.9 %all-to-all-start = ((f32[16,40,128]{2,1,0:T(8,128)}), f32[16,40,128]{2,1,0:T(8,128)}, u32[]{:S(2)}, u32[]{:S(2)}) async-start(f32[16,40,128]{2,1,0:T(8,128)} %bitcast.5), calls=%async_computation | async-start | bytes 655360 | tf_op jit(solution)/shard_map/all_to_all | solution.py:235
  60.4 5.2 %all-to-all-done = f32[16,40,128]{2,1,0:T(8,128)} async-done(((f32[16,40,128]{2,1,0:T(8,128)}), f32[16,40,128]{2,1,0:T(8,128)}, u32[]{:S(2)}, u32[]{:S(2)}) %all-to-all-start) | async-done | bytes 327712 | tf_op jit(solution)/shard_map/all_to_all | solution.py:235
  67.2 15.3 %all-to-all-start.1 = ((f32[8,40,128]{2,1,0:T(8,128)}), f32[8,40,128]{2,1,0:T(8,128)}, u32[]{:S(2)}, u32[]{:S(2)}) async-start(f32[8,40,128]{2,1,0:T(8,128)} %broadcast_in_dim.42), calls=%async_computation.1 | async-start | bytes 327680 | tf_op jit(solution)/shard_map/all_to_all | solution.py:235
  84.9 4.9 %collective-permute-start.7 = (f32[2,384,128]{2,1,0:T(8,128)}, f32[2,384,128]{2,1,0:T(8,128)}, u32[]{:S(2)}, u32[]{:S(2)}) collective-permute-start(f32[2,384,128]{2,1,0:T(8,128)} %get-tuple-element.26), channel_id=1, source_target_pairs={{1,2},{3,4},{5,6},{7,8},{9,10},{11,12},{13,14},{15,16},{17,18},{19... | collective-permute-start | bytes 1179656 | tf_op jit(solution)/shard_map/ppermute | solution.py:208
  92.7 4.0 %all-to-all-start.2 = ((f32[16,40,128]{2,1,0:T(8,128)}), f32[16,40,128]{2,1,0:T(8,128)S(1)}, u32[]{:S(2)}, u32[]{:S(2)}) async-start(f32[16,40,128]{2,1,0:T(8,128)} %broadcast_in_dim.43), calls=%async_computation.2 | async-start | bytes 655360 | tf_op jit(solution)/shard_map/all_to_all | solution.py:235
  97.6 2.8 %select_add_fusion.1 = f32[2,384,512]{2,1,0:T(8,128)} fusion(f32[2,384,384]{2,1,0:T(8,128)S(1)} %copy-done.10, pred[384,512]{1,0:T(8,128)(4,1)S(1)} %and_and_fusion, f32[2,384,128]{2,1,0:T(8,128)} %copy-done.16, f32[2,64,256]{2,1,0:T(8,128)} %copy-done.18, f32[2,256,256]{2,1,0:T(8,128)S(1)} %copy-done.12, f32[2,64,256]{2,1,0:T(8,128)} %copy-done.17, ...), kind=kLoop, calls=%fused_computation.2 | loop fusion | flops 2359296 | bytes 4521984 | tf_op jit(solution)/shard_map/add | solution.py:293
  100.3 2.2 %all-to-all-done.2 = f32[16,40,128]{2,1,0:T(8,128)S(1)} async-done(((f32[16,40,128]{2,1,0:T(8,128)}), f32[16,40,128]{2,1,0:T(8,128)S(1)}, u32[]{:S(2)}, u32[]{:S(2)}) %all-to-all-start.2) | async-done | bytes 327712 | tf_op jit(solution)/shard_map/all_to_all | solution.py:235
  102.5 3.7 %collective-permute-start.9 = (f32[640,128]{1,0:T(8,128)S(1)}, f32[640,128]{1,0:T(8,128)S(1)}, u32[]{:S(2)}, u32[]{:S(2)}) collective-permute-start(f32[640,128]{1,0:T(8,128)S(1)} %bitcast.16), channel_id=1, source_target_pairs={{0,1},{1,0},{2,3},{3,2},{4,5},{5,4},{6,7},{7,6},{8,9},{9,8},{10,11... | collective-permute-start | bytes 983048 | tf_op jit(solution)/shard_map/ppermute | solution.py:244
  107.4 2.7 %select_add_fusion.refs_3_ = f32[2,384,512]{2,1,0:T(8,128)} fusion(f32[2,384,512]{2,1,0:T(8,128)S(1)} %copy-done.13, f32[2,384,128]{2,1,0:T(8,128)S(1)} %get-tuple-element.15, f32[2,384,128]{2,1,0:T(8,128)S(1)} %get-tuple-element.14, pred[384,512]{1,0:T(8,128)(4,1)} %copy-done.19), kind=kLoop, calls=%fused_computation.1 | loop fusion | flops 1179648 | bytes 4128768 | tf_op jit(solution)/shard_map/add | solution.py:296
  110.1 6.5 %shard_map.114 = (f32[2,384,512]{2,1,0:T(8,128)S(1)}, f32[640,128]{1,0:T(8,128)S(1)}, f32[640,128]{1,0:T(8,128)S(1)}, f32[2,4,128,128]{3,2,1,0:T(8,128)S(1)}) custom-call(s32[8,2]{1,0:T(8,128)S(1)} %copy.14.refs_0_, s32[1]{0:T(128)} %bitcast.15.refs_1_, s32[1]{0:T(128)} %bitcast.2.refs_2_, f32[2,384,512]{2,1,0:T(8,128)} %select_add_fusion.refs_3_, ...), custom_call_target="tpu_custom_call" | custom-call | flops 6442450944 | bytes 6291456 | tf_op jit(solution)/shard_map/pallas_call | solution.py:191
  116.8 1.6 collective-permute-done.14
  119.1 9.9 %all-to-all-start.3 = ((f32[16,40,128]{2,1,0:T(8,128)}), f32[16,40,128]{2,1,0:T(8,128)S(1)}, u32[]{:S(2)}, u32[]{:S(2)}) async-start(f32[16,40,128]{2,1,0:T(8,128)} %bitcast.7), calls=%async_computation.3 | async-start | bytes 655360 | tf_op jit(solution)/shard_map/all_to_all | solution.py:235
  129.2 1.3 collective-permute-start.10
  131.2 4.6 %all-to-all-done.3 = f32[16,40,128]{2,1,0:T(8,128)S(1)} async-done(((f32[16,40,128]{2,1,0:T(8,128)}), f32[16,40,128]{2,1,0:T(8,128)S(1)}, u32[]{:S(2)}, u32[]{:S(2)}) %all-to-all-start.3) | async-done | bytes 327712 | tf_op jit(solution)/shard_map/all_to_all | solution.py:235
  136.5 4.8 %all-to-all-start.4 = ((f32[8,40,128]{2,1,0:T(8,128)}), f32[8,40,128]{2,1,0:T(8,128)S(1)}, u32[]{:S(2)}, u32[]{:S(2)}) async-start(f32[8,40,128]{2,1,0:T(8,128)} %broadcast_in_dim.44), calls=%async_computation.4 | async-start | bytes 327680 | tf_op jit(solution)/shard_map/all_to_all | solution.py:235
  141.6 9.3 %all-to-all-done.4 = f32[8,40,128]{2,1,0:T(8,128)S(1)} async-done(((f32[8,40,128]{2,1,0:T(8,128)}), f32[8,40,128]{2,1,0:T(8,128)S(1)}, u32[]{:S(2)}, u32[]{:S(2)}) %all-to-all-start.4) | async-done | bytes 163872 | tf_op jit(solution)/shard_map/all_to_all | solution.py:235
  151.7 6.8 %all-to-all-start.5 = ((f32[16,40,128]{2,1,0:T(8,128)}), f32[16,40,128]{2,1,0:T(8,128)S(1)}, u32[]{:S(2)}, u32[]{:S(2)}) async-start(f32[16,40,128]{2,1,0:T(8,128)} %broadcast_in_dim.45), calls=%async_computation.5 | async-start | bytes 655360 | tf_op jit(solution)/shard_map/all_to_all | solution.py:235
  158.6 2.1 %collective-permute-start.12 = (f32[2,256,64]{2,1,0:T(8,128)S(1)}, f32[2,256,64]{2,1,0:T(8,128)S(1)}, u32[]{:S(2)}, u32[]{:S(2)}) collective-permute-start(f32[2,256,64]{2,1,0:T(8,128)S(1)} %get-tuple-element.28), channel_id=1, source_target_pairs={{0,1},{2,3},{4,5},{6,7},{8,9},{10,11},{12,13},{14,15},{16,17},{18,... | collective-permute-start | bytes 393224 | tf_op jit(solution)/shard_map/ppermute | solution.py:208
  160.8 1.9 %collective-permute-start.13 = (f32[2,256,64]{2,1,0:T(8,128)S(1)}, f32[2,256,64]{2,1,0:T(8,128)S(1)}, u32[]{:S(2)}, u32[]{:S(2)}) collective-permute-start(f32[2,256,64]{2,1,0:T(8,128)S(1)} %get-tuple-element.29), channel_id=1, source_target_pairs={{1,2},{3,4},{5,6},{7,8},{9,10},{11,12},{13,14},{15,16},{17,18},{19... | collective-permute-start | bytes 393224 | tf_op jit(solution)/shard_map/ppermute | solution.py:208
  162.7 1.7 all-to-all-done.5
  164.4 2.8 %collective-permute-start.15 = (f32[640,128]{1,0:T(8,128)S(1)}, f32[640,128]{1,0:T(8,128)S(1)}, u32[]{:S(2)}, u32[]{:S(2)}) collective-permute-start(f32[640,128]{1,0:T(8,128)S(1)} %bitcast.19), channel_id=1, source_target_pairs={{0,1},{1,0},{2,3},{3,2},{4,5},{5,4},{6,7},{7,6},{8,9},{9,8},{10,11... | collective-permute-start | bytes 983048 | tf_op jit(solution)/shard_map/ppermute | solution.py:244
  167.2 3.3 %collective-permute-done.13 = f32[2,256,64]{2,1,0:T(8,128)S(1)} collective-permute-done((f32[2,256,64]{2,1,0:T(8,128)S(1)}, f32[2,256,64]{2,1,0:T(8,128)S(1)}, u32[]{:S(2)}, u32[]{:S(2)}) %collective-permute-start.13) | collective-permute-done | bytes 131104 | tf_op jit(solution)/shard_map/ppermute | solution.py:208
  170.6 2.1 %fusion.1 = f32[2,256,256]{2,1,0:T(8,128)} fusion(f32[2,256,384]{2,1,0:T(8,128)S(1)} %pad_add_fusion.1, f32[2,384,512]{2,1,0:T(8,128)} %select_add_fusion.refs_3_, f32[2,256,64]{2,1,0:T(8,128)S(1)} %get-tuple-element.41, f32[2,256,64]{2,1,0:T(8,128)S(1)} %get-tuple-element.40), kind=kLoop, calls=%fused_computation.10 | loop fusion | flops 393216 | bytes 1835008 | tf_op jit(solution)/shard_map/add | solution.py:309
  (98 shorter events, 20.7 us)
Async XLA Ops:
  1.6 4.5 %collective-permute-start = (f32[2,64,256]{2,1,0:T(8,128)S(1)}, f32[2,64,256]{2,1,0:T(8,128)S(1)}, u32[]{:S(2)}, u32[]{:S(2)}) collective-permute-start(f32[2,64,256]{2,1,0:T(8,128)S(1)} %get-tuple-element.42), channel_id=1, source_target_pairs={{0,32},{64,96},{128,160},{192,224},{32,0},{96,64},{160,128},{224,1... | collective-permute-start | bytes 393224 | tf_op jit(solution)/shard_map/ppermute | solution.py:208
  2.9 3.2 %collective-permute-start.1 = (f32[2,64,256]{2,1,0:T(8,128)S(1)}, f32[2,64,256]{2,1,0:T(8,128)S(1)}, u32[]{:S(2)}, u32[]{:S(2)}) collective-permute-start(f32[2,64,256]{2,1,0:T(8,128)S(1)} %get-tuple-element.43), channel_id=1, source_target_pairs={{32,64},{96,128},{160,192},{64,32},{128,96},{192,160},{33,65},{97,... | collective-permute-start | bytes 393224 | tf_op jit(solution)/shard_map/ppermute | solution.py:208
  6.1 14.2 %copy-start.17 = (f32[2,64,256]{2,1,0:T(8,128)}, f32[2,64,256]{2,1,0:T(8,128)S(1)}, u32[]{:S(2)}) copy-start(f32[2,64,256]{2,1,0:T(8,128)S(1)} %get-tuple-element.46) | copy-start | bytes 393220
  6.2 14.2 %copy-start.18 = (f32[2,64,256]{2,1,0:T(8,128)}, f32[2,64,256]{2,1,0:T(8,128)S(1)}, u32[]{:S(2)}) copy-start(f32[2,64,256]{2,1,0:T(8,128)S(1)} %get-tuple-element.47) | copy-start | bytes 393220
  6.2 6.2 %copy-start.22 = (s32[1,1,8,2]{2,3,1,0:T(2,128)S(1)}, s32[1,1,8,2]{2,3,1,0:T(2,128)}, u32[]{:S(2)}) copy-start(s32[1,1,8,2]{2,3,1,0:T(2,128)} %param.14) | copy-start | bytes 196
  6.2 6.9 %copy-start.20 = (bf16[1,1,8,128,128]{4,3,2,1,0:T(8,128)(2,1)S(1)}, bf16[1,1,8,128,128]{4,3,2,1,0:T(8,128)(2,1)}, u32[]{:S(2)}) copy-start(bf16[1,1,8,128,128]{4,3,2,1,0:T(8,128)(2,1)} %param.12) | copy-start | bytes 786436
  6.2 6.9 %copy-start.21 = (f32[1,1,8,128]{3,2,1,0:T(8,128)S(1)}, f32[1,1,8,128]{3,2,1,0:T(8,128)}, u32[]{:S(2)}) copy-start(f32[1,1,8,128]{3,2,1,0:T(8,128)} %param.13) | copy-start | bytes 12292
  7.5 12.9 %copy-start.11 = (f32[2,256,256]{2,1,0:T(8,128)S(1)}, f32[2,256,256]{2,1,0:T(8,128)}, u32[]{:S(2)}) copy-start(f32[2,256,256]{2,1,0:T(8,128)} %param.10) | copy-start | bytes 1572868
  7.5 5.8 %collective-permute-start.2 = (f32[2,384,128]{2,1,0:T(8,128)S(1)}, f32[2,384,128]{2,1,0:T(8,128)S(1)}, u32[]{:S(2)}, u32[]{:S(2)}) collective-permute-start(f32[2,384,128]{2,1,0:T(8,128)S(1)} %get-tuple-element.36), channel_id=1, source_target_pairs={{0,1},{2,3},{4,5},{6,7},{8,9},{10,11},{12,13},{14,15},{16,17},{18,... | collective-permute-start | bytes 1179656 | tf_op jit(solution)/shard_map/ppermute | solution.py:208
  9.1 11.2 %collective-permute-start.3 = (f32[2,384,128]{2,1,0:T(8,128)S(1)}, f32[2,384,128]{2,1,0:T(8,128)S(1)}, u32[]{:S(2)}, u32[]{:S(2)}) collective-permute-start(f32[2,384,128]{2,1,0:T(8,128)S(1)} %get-tuple-element.37), channel_id=1, source_target_pairs={{1,2},{3,4},{5,6},{7,8},{9,10},{11,12},{13,14},{15,16},{17,18},{19... | collective-permute-start | bytes 1179656 | tf_op jit(solution)/shard_map/ppermute | solution.py:208
  27.5 11.0 %collective-permute-start.8 = (f32[640,128]{1,0:T(8,128)S(1)}, f32[640,128]{1,0:T(8,128)}, u32[]{:S(2)}, u32[]{:S(2)}) collective-permute-start(f32[640,128]{1,0:T(8,128)S(1)} %get-tuple-element.17), channel_id=1, source_target_pairs={{0,1},{1,0},{2,3},{3,2},{4,5},{5,4},{6,7},{7,6},{8,9},{9,8},{10,11... | collective-permute-start | bytes 983048 | tf_op jit(solution)/shard_map/ppermute | solution.py:244
  28.7 30.5 %collective-permute-start.4 = (f32[2,128,384]{2,1,0:T(8,128)}, f32[2,128,384]{2,1,0:T(8,128)}, u32[]{:S(2)}, u32[]{:S(2)}) collective-permute-start(f32[2,128,384]{2,1,0:T(8,128)} %get-tuple-element.24), channel_id=1, source_target_pairs={{0,32},{64,96},{128,160},{192,224},{32,0},{96,64},{160,128},{224,1... | collective-permute-start | bytes 1179656 | tf_op jit(solution)/shard_map/ppermute | solution.py:208
  37.1 22.1 %collective-permute-start.5 = (f32[2,128,384]{2,1,0:T(8,128)}, f32[2,128,384]{2,1,0:T(8,128)}, u32[]{:S(2)}, u32[]{:S(2)}) collective-permute-start(f32[2,128,384]{2,1,0:T(8,128)} %get-tuple-element.25), channel_id=1, source_target_pairs={{32,64},{96,128},{160,192},{64,32},{128,96},{192,160},{33,65},{97,... | collective-permute-start | bytes 1179656 | tf_op jit(solution)/shard_map/ppermute | solution.py:208
  40.2 25.3 %all-to-all-start = ((f32[16,40,128]{2,1,0:T(8,128)}), f32[16,40,128]{2,1,0:T(8,128)}, u32[]{:S(2)}, u32[]{:S(2)}) async-start(f32[16,40,128]{2,1,0:T(8,128)} %bitcast.5), calls=%async_computation | async-start | bytes 655360 | tf_op jit(solution)/shard_map/all_to_all | solution.py:235
  67.2 23.8 %all-to-all-start.1 = ((f32[8,40,128]{2,1,0:T(8,128)}), f32[8,40,128]{2,1,0:T(8,128)}, u32[]{:S(2)}, u32[]{:S(2)}) async-start(f32[8,40,128]{2,1,0:T(8,128)} %broadcast_in_dim.42), calls=%async_computation.1 | async-start | bytes 327680 | tf_op jit(solution)/shard_map/all_to_all | solution.py:235
  83.9 13.6 %copy-start.12 = (f32[2,256,256]{2,1,0:T(8,128)S(1)}, f32[2,256,256]{2,1,0:T(8,128)}, u32[]{:S(2)}) copy-start(f32[2,256,256]{2,1,0:T(8,128)} %param.10) | copy-start | bytes 1572868
  83.9 13.6 %copy-start.15 = (f32[2,384,128]{2,1,0:T(8,128)S(1)}, f32[2,384,128]{2,1,0:T(8,128)}, u32[]{:S(2)}) copy-start(f32[2,384,128]{2,1,0:T(8,128)} %copy-done.14) | copy-start | bytes 1179652
  84.9 12.7 %copy-start.10 = (f32[2,384,384]{2,1,0:T(8,128)S(1)}, f32[2,384,384]{2,1,0:T(8,128)}, u32[]{:S(2)}) copy-start(f32[2,384,384]{2,1,0:T(8,128)} %copy-done.9) | copy-start | bytes 3538948
  84.9 21.3 %collective-permute-start.7 = (f32[2,384,128]{2,1,0:T(8,128)}, f32[2,384,128]{2,1,0:T(8,128)}, u32[]{:S(2)}, u32[]{:S(2)}) collective-permute-start(f32[2,384,128]{2,1,0:T(8,128)} %get-tuple-element.26), channel_id=1, source_target_pairs={{1,2},{3,4},{5,6},{7,8},{9,10},{11,12},{13,14},{15,16},{17,18},{19... | collective-permute-start | bytes 1179656 | tf_op jit(solution)/shard_map/ppermute | solution.py:208
  89.8 16.4 %collective-permute-start.6 = (f32[2,384,128]{2,1,0:T(8,128)}, f32[2,384,128]{2,1,0:T(8,128)}, u32[]{:S(2)}, u32[]{:S(2)}) collective-permute-start(f32[2,384,128]{2,1,0:T(8,128)} %get-tuple-element.27), channel_id=1, source_target_pairs={{0,1},{2,3},{4,5},{6,7},{8,9},{10,11},{12,13},{14,15},{16,17},{18,... | collective-permute-start | bytes 1179656 | tf_op jit(solution)/shard_map/ppermute | solution.py:208
  92.7 9.8 %all-to-all-start.2 = ((f32[16,40,128]{2,1,0:T(8,128)}), f32[16,40,128]{2,1,0:T(8,128)S(1)}, u32[]{:S(2)}, u32[]{:S(2)}) async-start(f32[16,40,128]{2,1,0:T(8,128)} %broadcast_in_dim.43), calls=%async_computation.2 | async-start | bytes 655360 | tf_op jit(solution)/shard_map/all_to_all | solution.py:235
  100.3 7.1 %copy-start.13 = (f32[2,384,512]{2,1,0:T(8,128)S(1)}, f32[2,384,512]{2,1,0:T(8,128)}, u32[]{:S(2)}) copy-start(f32[2,384,512]{2,1,0:T(8,128)} %select_add_fusion.1) | copy-start | bytes 4718596
  102.5 7.6 %collective-permute-start.9 = (f32[640,128]{1,0:T(8,128)S(1)}, f32[640,128]{1,0:T(8,128)S(1)}, u32[]{:S(2)}, u32[]{:S(2)}) collective-permute-start(f32[640,128]{1,0:T(8,128)S(1)} %bitcast.16), channel_id=1, source_target_pairs={{0,1},{1,0},{2,3},{3,2},{4,5},{5,4},{6,7},{7,6},{8,9},{9,8},{10,11... | collective-permute-start | bytes 983048 | tf_op jit(solution)/shard_map/ppermute | solution.py:244
  116.7 1.7 collective-permute-start.14
  119.1 16.6 %all-to-all-start.3 = ((f32[16,40,128]{2,1,0:T(8,128)}), f32[16,40,128]{2,1,0:T(8,128)S(1)}, u32[]{:S(2)}, u32[]{:S(2)}) async-start(f32[16,40,128]{2,1,0:T(8,128)} %bitcast.7), calls=%async_computation.3 | async-start | bytes 655360 | tf_op jit(solution)/shard_map/all_to_all | solution.py:235
  129.2 12.1 %collective-permute-start.10 = (f32[2,64,384]{2,1,0:T(8,128)S(1)}, f32[2,64,384]{2,1,0:T(8,128)S(1)}, u32[]{:S(2)}, u32[]{:S(2)}) collective-permute-start(f32[2,64,384]{2,1,0:T(8,128)S(1)} %get-tuple-element.22), channel_id=1, source_target_pairs={{0,32},{64,96},{128,160},{192,224},{32,0},{96,64},{160,128},{224,1... | collective-permute-start | bytes 589832 | tf_op jit(solution)/shard_map/ppermute | solution.py:208
  130.5 10.8 %collective-permute-start.11 = (f32[2,64,384]{2,1,0:T(8,128)S(1)}, f32[2,64,384]{2,1,0:T(8,128)S(1)}, u32[]{:S(2)}, u32[]{:S(2)}) collective-permute-start(f32[2,64,384]{2,1,0:T(8,128)S(1)} %get-tuple-element.23), channel_id=1, source_target_pairs={{32,64},{96,128},{160,192},{64,32},{128,96},{192,160},{33,65},{97,... | collective-permute-start | bytes 589832 | tf_op jit(solution)/shard_map/ppermute | solution.py:208
  136.5 14.4 %all-to-all-start.4 = ((f32[8,40,128]{2,1,0:T(8,128)}), f32[8,40,128]{2,1,0:T(8,128)S(1)}, u32[]{:S(2)}, u32[]{:S(2)}) async-start(f32[8,40,128]{2,1,0:T(8,128)} %broadcast_in_dim.44), calls=%async_computation.4 | async-start | bytes 327680 | tf_op jit(solution)/shard_map/all_to_all | solution.py:235
  151.7 12.7 %all-to-all-start.5 = ((f32[16,40,128]{2,1,0:T(8,128)}), f32[16,40,128]{2,1,0:T(8,128)S(1)}, u32[]{:S(2)}, u32[]{:S(2)}) async-start(f32[16,40,128]{2,1,0:T(8,128)} %broadcast_in_dim.45), calls=%async_computation.5 | async-start | bytes 655360 | tf_op jit(solution)/shard_map/all_to_all | solution.py:235
  158.6 8.6 %collective-permute-start.12 = (f32[2,256,64]{2,1,0:T(8,128)S(1)}, f32[2,256,64]{2,1,0:T(8,128)S(1)}, u32[]{:S(2)}, u32[]{:S(2)}) collective-permute-start(f32[2,256,64]{2,1,0:T(8,128)S(1)} %get-tuple-element.28), channel_id=1, source_target_pairs={{0,1},{2,3},{4,5},{6,7},{8,9},{10,11},{12,13},{14,15},{16,17},{18,... | collective-permute-start | bytes 393224 | tf_op jit(solution)/shard_map/ppermute | solution.py:208
  160.8 9.8 %collective-permute-start.13 = (f32[2,256,64]{2,1,0:T(8,128)S(1)}, f32[2,256,64]{2,1,0:T(8,128)S(1)}, u32[]{:S(2)}, u32[]{:S(2)}) collective-permute-start(f32[2,256,64]{2,1,0:T(8,128)S(1)} %get-tuple-element.29), channel_id=1, source_target_pairs={{1,2},{3,4},{5,6},{7,8},{9,10},{11,12},{13,14},{15,16},{17,18},{19... | collective-permute-start | bytes 393224 | tf_op jit(solution)/shard_map/ppermute | solution.py:208
  164.4 8.3 %collective-permute-start.15 = (f32[640,128]{1,0:T(8,128)S(1)}, f32[640,128]{1,0:T(8,128)S(1)}, u32[]{:S(2)}, u32[]{:S(2)}) collective-permute-start(f32[640,128]{1,0:T(8,128)S(1)} %bitcast.19), channel_id=1, source_target_pairs={{0,1},{1,0},{2,3},{3,2},{4,5},{5,4},{6,7},{7,6},{8,9},{9,8},{10,11... | collective-permute-start | bytes 983048 | tf_op jit(solution)/shard_map/ppermute | solution.py:244
  (13 other events, 20.9 us)
